TPU v7x, 32 devices: a whole 2x2x4 slice. The times are simulated.
32 devices in a mesh: grp: 4 (over x, core), tp: 4 (over z), cores: 2 (over y).
Axes of the slice: x: 2, y: 2, z: 4, core: 2. Of those that a mesh axis runs over, the one named last changes fastest.
Arguments:
- tokens: bfloat16 [4096, 8192], P('grp', ('tp', 'cores')), may hold values from -6 to 6
- gate_up_weight: bfloat16 [8192, 2, 16384], P(None, None, ('tp', 'cores')), may hold values from -0.0625 to 0.0625
- down_factor_pool: bfloat16 [8, 8192, 256], P(('tp', 'cores'), 'grp'), may hold values from -0.0625 to 0.0625
- up_factor_pool: bfloat16 [8, 4, 8, 128, 1024], P(('tp', 'cores'), 'grp'), may hold values from -0.5 to 0.5
- segment_adapters: int32 [4, 3], replicated, may hold values from 0 to 7
- segment_tile_counts: int32 [4, 3], P('grp'), may hold values from 1 to 4, 8 in all within a row
- adapter_pool_rows: int32 [8], replicated, may hold values from 0 to 7, each once
Outputs:
- hidden: bfloat16 [4096, 16384], P('grp', ('tp', 'cores'))
Inputs may be any that keep to these rules, and one draw needn't show every extreme that they name: `segment_tile_counts`: each row sums to 8. `adapter_pool_rows`: each pool row appears once.
All inputs are finite; a program needn't handle non-finite values.
Results may differ from a plain program's by a relative error of at most 0.0036.
Values may be sent and summed in bfloat16 or wider, within the bound.
A program may use at most 320 MiB of HBM per device.

v0:
```python
import functools

import jax
import jax.numpy as jnp
from jax import lax
from jax.experimental import pallas as pl
from jax.experimental.pallas import tpu as pltpu
from jax.sharding import PartitionSpec as P


TILE = 128
VMEM_LIMIT = 60 * 1024 * 1024

adapter_scale = 0.5


TP = ("tp", "cores")


def tile_segments(tile_lengths, tile_count):
    bounds = jnp.cumsum(tile_lengths)
    positions = jnp.arange(tile_count, dtype=jnp.int32)
    return jnp.sum((bounds[None, :] <= positions[:, None]).astype(jnp.int32), axis=1)


def ring_device(position, tp_size, cores_size):
    c = position // tp_size
    t = position % tp_size
    t = t + (c % 2) * (tp_size - 1 - 2 * t)
    return t * cores_size + c


def ring_position(tp_index, cores_index, tp_size):
    t = tp_index + (cores_index % 2) * (tp_size - 1 - 2 * tp_index)
    return cores_index * tp_size + t


def partial_kernel(count, with_acc, rows_ref, *refs):
    xs, ws = refs[:count], refs[count : 2 * count]
    out = refs[-1]
    ws = [jnp.swapaxes(w[...], 0, 1) for w in ws]
    for h in range(2):
        total = refs[2 * count][h] if with_acc else None
        for x, w in zip(xs, ws):
            term = jnp.dot(x[...], w[h], preferred_element_type=jnp.float32)
            total = term if total is None else total + term
        out[h] = total


def partial_matmul(xs, weight, rows, acc, block_cols):
    count = len(xs)
    tokens, depth = xs[0].shape
    hidden = weight.shape[2]
    block_cols = min(block_cols, 256)
    in_specs = [pl.BlockSpec((tokens, depth), lambda j, r: (0, 0))] * count
    for k in range(count):
        in_specs.append(
            pl.BlockSpec((depth, 2, block_cols), lambda j, r, k=k: (r[k], 0, j))
        )
    acc_spec = pl.BlockSpec((2, tokens, block_cols), lambda j, r: (0, 0, j))
    operands = list(xs) + [weight] * count
    aliases = {}
    if acc is not None:
        in_specs.append(acc_spec)
        aliases = {1 + len(operands): 0}
        operands.append(acc)
    return pl.pallas_call(
        functools.partial(partial_kernel, count, acc is not None),
        out_shape=jax.ShapeDtypeStruct((2, tokens, hidden), jnp.float32),
        grid_spec=pltpu.PrefetchScalarGridSpec(
            num_scalar_prefetch=1,
            grid=(hidden // block_cols,),
            in_specs=in_specs,
            out_specs=acc_spec,
        ),
        input_output_aliases=aliases,
        compiler_params=pltpu.CompilerParams(vmem_limit_bytes=VMEM_LIMIT),
        cost_estimate=pl.CostEstimate(
            flops=4 * count * tokens * depth * hidden,
            bytes_accessed=count * 4 * depth * hidden + 16 * tokens * hidden,
            transcendentals=0,
        ),
    )(rows, *operands)


def final_kernel(tiles_per_half, rank, rows_ref, seg_ref, xt, xb, w, acc, shrunk, b, out, total):
    narrow = out.shape[1]
    w = jnp.swapaxes(w[...], 0, 1)
    for p, x in enumerate((xt, xb)):
        for h in range(2):
            span = slice(p * x.shape[0], (p + 1) * x.shape[0])
            total[h, span] = acc[h, span] + jnp.dot(
                x[...], w[h], preferred_element_type=jnp.float32
            )
        for t in range(p * tiles_per_half, (p + 1) * tiles_per_half):
            seg = seg_ref[t]
            span = slice(t * TILE, (t + 1) * TILE)
            both = []
            for h in range(2):
                delta = jnp.dot(
                    shrunk[span, h * rank : (h + 1) * rank],
                    b[0, seg, :, h * narrow : (h + 1) * narrow],
                    preferred_element_type=jnp.float32,
                )
                both.append(total[h, span] + adapter_scale * delta)
            gate, up = both
            out[span] = (gate / (1.0 + jnp.exp(-gate)) * up).astype(out.dtype)


def final_matmul(xt, xb, weight, rows, acc, shrunk, b_chosen, tile_seg):
    half, depth = xt.shape
    tokens = 2 * half
    hidden = weight.shape[2]
    blocks, segs, rank, twice = b_chosen.shape
    narrow = twice // 2
    return pl.pallas_call(
        functools.partial(final_kernel, half // TILE, rank),
        out_shape=jax.ShapeDtypeStruct((tokens, hidden), jnp.bfloat16),
        grid_spec=pltpu.PrefetchScalarGridSpec(
            num_scalar_prefetch=2,
            grid=(blocks,),
            in_specs=[
                pl.BlockSpec((half, depth), lambda j, r, s: (0, 0)),
                pl.BlockSpec((half, depth), lambda j, r, s: (0, 0)),
                pl.BlockSpec((depth, 2, narrow), lambda j, r, s: (r[0], 0, j)),
                pl.BlockSpec((2, tokens, narrow), lambda j, r, s: (0, 0, j)),
                pl.BlockSpec((tokens, 2 * rank), lambda j, r, s: (0, 0)),
                pl.BlockSpec((1, segs, rank, twice), lambda j, r, s: (j, 0, 0, 0)),
            ],
            out_specs=pl.BlockSpec((tokens, narrow), lambda j, r, s: (0, j)),
            scratch_shapes=[pltpu.VMEM((2, tokens, narrow), jnp.float32)],
        ),
        compiler_params=pltpu.CompilerParams(vmem_limit_bytes=VMEM_LIMIT),
        cost_estimate=pl.CostEstimate(
            flops=4 * tokens * (depth + rank) * hidden,
            bytes_accessed=4 * depth * hidden + 10 * tokens * hidden,
            transcendentals=tokens * hidden,
        ),
    )(rows, tile_seg, xt, xb, weight, acc, shrunk, b_chosen)


def group_exchange(pool, slots):
    groups = lax.axis_size("grp")
    g = lax.axis_index("grp")
    parts = []
    for k in range(groups):
        wanted = lax.dynamic_index_in_dim(slots, (g + k) % groups, 0, keepdims=False)
        part = jnp.take(pool, wanted, axis=0, mode="clip")
        if k:
            pairs = [(i, (i + k) % groups) for i in range(groups)]
            part = lax.ppermute(part, "grp", pairs)
        parts.append(part)
    sources = (g + groups - jnp.arange(groups)) % groups
    return jnp.take(jnp.stack(parts), sources, axis=0, mode="clip")


MESH = pl.DeviceIdType.MESH
CHUNKS = 4
END_SHIFT = 1
BLOCK_COLS = 256


def table(rows, i, k):
    total = 0
    for a, row in enumerate(rows):
        for b, value in enumerate(row):
            if value:
                total = total + jnp.where((i == a) & (k == b), value, 0)
    return total


def reach(size):
    return [sorted(range(size), key=lambda t, z=z: (abs(t - z), t)) for z in range(size)]


def shifted(size, source, dest, c):
    to_end = ((dest == 0) | (dest == size - 1)) & (c >= CHUNKS - END_SHIFT)
    from_end = (source == 0) | (source == size - 1)
    return to_end | from_end


def gather_kernel(
    tile_rows,
    tokens,
    weight,
    down,
    up,
    xg,
    u_all,
    shrunk,
    acc_out,
    acc,
    xv,
    wbuf,
    d0,
    d_all,
    part,
    sums,
    own,
    recv,
    up_sem,
    dn_sem,
    y_sem,
    x_sem,
    w_sem,
    d0_send,
    d0_recv,
    d1_send,
    d1_recv,
    d2_send,
    d2_recv,
    u1_send,
    u1_recv,
    u2_send,
    u2_recv,
    s1_send,
    s1_recv,
    s2_send,
    s2_recv,
    o_sem,
):
    groups = lax.axis_size("grp")
    size, cores = lax.axis_size("tp"), lax.axis_size("cores")
    n = size * cores
    g, z, y = lax.axis_index("grp"), lax.axis_index("tp"), lax.axis_index("cores")
    me = z * cores + y
    other = 1 - y
    token_count, depth = tokens.shape
    rows = token_count // CHUNKS
    hidden = weight.shape[2]
    cols = wbuf.shape[-1]
    blocks = hidden // cols
    per = n // groups
    share = token_count // n
    order = reach(size)

    def peer(k):
        return {"grp": lax.rem(g + k, groups)}

    def mate(k):
        p = lax.rem(me + k, n)
        return p, {"tp": p // cores, "cores": lax.rem(p, cores)}

    def span(c):
        if isinstance(c, int):
            return pl.ds(c * rows, rows)
        return pl.ds(pl.multiple_of(c * rows, rows), rows)

    def hop(src, s, c, sems, dev):
        return pltpu.make_async_remote_copy(
            src_ref=src,
            dst_ref=xg.at[s, span(c)],
            send_sem=sems.at[s, c],
            recv_sem=recv.at[s, c],
            device_id=dev,
            device_id_type=MESH,
        )

    up_dev, dn_dev, y_dev = {"tp": z + 1}, {"tp": z - 1}, {"cores": other}

    def arrived(s, c):
        hop(xg.at[s, span(c)], s, c, y_sem, y_dev).wait_recv()

    def forward(s, c, sems, dev):
        hop(xg.at[s, span(c)], s, c, sems, dev).start()

    def send_own(c):
        src = tokens.at[span(c)]

        @pl.when(z + 1 < size)
        def _():
            hop(src, me, c, up_sem, up_dev).start()

        @pl.when(z >= 1)
        def _():
            hop(src, me, c, dn_sem, dn_dev).start()

        hop(src, me, c, y_sem, y_dev).start()

    def row_arrival(r, c, first):
        lo, hi = z - r, z + r

        @pl.when(lo >= 0)
        def _():
            s = lo * cores + y
            arrived(s, c)

            @pl.when(z + 1 < size)
            def _():
                forward(s, c, up_sem, up_dev)

            @pl.when(jnp.logical_not(shifted(size, lo, z, c)) if first else z >= 0)
            def _():
                forward(s, c, y_sem, y_dev)

        @pl.when(hi < size)
        def _():
            s = hi * cores + y
            arrived(s, c)

            @pl.when(z >= 1)
            def _():
                forward(s, c, dn_sem, dn_dev)

            @pl.when(jnp.logical_not(shifted(size, hi, z, c)) if first else z >= 0)
            def _():
                forward(s, c, y_sem, y_dev)

    def cross_arrival(r, c):
        lo, hi = z - r, z + r

        @pl.when(lo >= 0)
        def _():
            arrived(lo * cores + other, c)

        @pl.when(hi < size)
        def _():
            arrived(hi * cores + other, c)

    def mate_arrival(c):
        s = z * cores + other
        arrived(s, c)

        @pl.when((z + 1 < size) & shifted(size, z, z + 1, c))
        def _():
            forward(s, c, up_sem, up_dev)

        @pl.when((z >= 1) & shifted(size, z, z - 1, c))
        def _():
            forward(s, c, dn_sem, dn_dev)

    def w_copy(piece, j, slot, k):
        return pltpu.make_async_copy(
            weight.at[
                pl.ds(pl.multiple_of(piece * depth, depth), depth),
                slice(None),
                pl.ds(pl.multiple_of(j * cols, cols), cols),
            ],
            wbuf.at[slot, k],
            w_sem.at[slot, k],
        )

    def x_copy(src, k):
        return pltpu.make_async_copy(src, xv.at[k], x_sem.at[k])

    def multiply(pieces, j, count, first):
        slot = lax.rem(j, 2)

        @pl.when(j + 1 < blocks)
        def _():
            for k, piece in enumerate(pieces):
                w_copy(piece, j + 1, 1 - slot, k).start()

        where = pl.ds(pl.multiple_of(j * cols, cols), cols)
        for k, piece in enumerate(pieces):
            w_copy(piece, j, slot, k).wait()
        ws = [jnp.swapaxes(wbuf[slot, k], 0, 1) for k in range(len(pieces))]
        for h in range(2):
            total = None if first else acc[h, pl.ds(0, count), where]
            for k in range(len(pieces)):
                term = jnp.dot(
                    xv[k, pl.ds(0, count)], ws[k][h], preferred_element_type=jnp.float32
                )
                total = term if total is None else total + term
            acc[h, pl.ds(0, count), where] = total

    def first_tiles(pieces):
        for k, piece in enumerate(pieces):
            w_copy(piece, 0, 0, k).start()

    def exchange(k, src, dst, sends, recvs, dev):
        return pltpu.make_async_remote_copy(
            src_ref=src,
            dst_ref=dst,
            send_sem=sends.at[k],
            recv_sem=recvs.at[k],
            device_id=dev,
            device_id_type=MESH,
        )

    def d0_copy(k):
        return exchange(
            k, down.at[:, lax.rem(g + k, groups)], d0.at[g], d0_send, d0_recv, peer(k)
        )

    def d1_copy(k):
        p, dev = mate(k)
        return exchange(
            k, d0.at[p // per, lax.rem(p, per)], d_all.at[g, me], d1_send, d1_recv, dev
        )

    def d2_copy(k):
        return exchange(k, d_all.at[g], d_all.at[g], d2_send, d2_recv, peer(k))

    def u1_copy(k):
        p, dev = mate(k)
        return exchange(k, up.at[p], u_all.at[g, me], u1_send, u1_recv, dev)

    def u2_copy(k):
        return exchange(k, u_all.at[g], u_all.at[g], u2_send, u2_recv, peer(k))

    def s1_copy(k):
        p, dev = mate(k)
        src = part.at[pl.ds(pl.multiple_of(p * share, share), share)]
        return exchange(k, src, sums.at[me], s1_send, s1_recv, dev)

    def s2_copy(k):
        _, dev = mate(k)
        return exchange(k, own, shrunk.at[me], s2_send, s2_recv, dev)

    def here(src, dst, k):
        return pltpu.make_async_copy(src, dst, o_sem.at[k])

    for k in range(1, groups):
        d0_copy(k).start()
    here(down.at[:, g], d0.at[g], 0).start()
    x_copy(tokens, 0).start()
    first_tiles([me])
    send_own(0)
    here(down.at[:, g], d0.at[g], 0).wait()
    for k in range(1, groups):
        d0_copy(k).wait_recv()
    for k in range(1, n):
        d1_copy(k).start()
    here(d0.at[me // per, lax.rem(me, per)], d_all.at[g, me], 1).start()
    for c in range(1, CHUNKS):
        send_own(c)
    for k in range(1, n):
        u1_copy(k).start()
    here(up.at[me], u_all.at[g, me], 2).start()
    x_copy(tokens, 0).wait()

    step = blocks // CHUNKS

    def first_round(c, carry):
        row_arrival(1, c, True)
        mate_arrival(c)
        for i in range(step):
            multiply([me], c * step + i, token_count, True)
        return carry

    lax.fori_loop(0, CHUNKS, first_round, 0)

    here(d0.at[me // per, lax.rem(me, per)], d_all.at[g, me], 1).wait()
    for k in range(1, n):
        d1_copy(k).wait_recv()
    for k in range(1, groups):
        d2_copy(k).start()
    here(up.at[me], u_all.at[g, me], 2).wait()
    for k in range(1, n):
        u1_copy(k).wait_recv()
    for k in range(1, groups):
        u2_copy(k).start()

    def later_round(r, carry):
        pieces = [
            table(order, z, r - 1) * cores + y,
            table(order, z, r - 2) * cores + other,
        ]
        for k in range(2):
            x_copy(xg.at[pieces[k]], k).start()
        first_tiles(pieces)
        for k in range(2):
            x_copy(xg.at[pieces[k]], k).wait()

        def body(c, carry):
            @pl.when(r < size)
            def _():
                row_arrival(r, c, False)
                cross_arrival(r - 1, c)

            for i in range(step):
                multiply(pieces, c * step + i, token_count, False)
            return carry

        lax.fori_loop(0, CHUNKS, body, 0)

        @pl.when(r == 2)
        def _():
            for k in range(1, groups):
                d2_copy(k).wait_recv()
            x_copy(tokens, 0).start()
            x_copy(tokens, 0).wait()

            def one_tile(t, carry):
                q = tile_rows[t]
                where = pl.ds(pl.multiple_of(t * TILE, TILE), TILE)
                piece = depth // groups
                total = None
                for j in range(groups):
                    term = jnp.dot(
                        xv[0, where, j * piece : (j + 1) * piece],
                        d_all[j, q],
                        preferred_element_type=jnp.float32,
                    )
                    total = term if total is None else total + term
                part[where] = total.astype(part.dtype)
                return carry

            lax.fori_loop(0, token_count // TILE, one_tile, 0)
            for k in range(1, n):
                s1_copy(k).start()

        @pl.when(r == 3)
        def _():
            for k in range(1, n):
                s1_copy(k).wait_recv()
            mine = part[pl.ds(pl.multiple_of(me * share, share), share)].astype(jnp.float32)
            for k in range(1, n):
                mine = mine + sums[lax.rem(me + k, n)].astype(jnp.float32)
            own[...] = mine.astype(own.dtype)
            here(own, shrunk.at[me], 3).start()
            for k in range(1, n):
                s2_copy(k).start()

        return carry

    lax.fori_loop(2, size + 1, later_round, 0)

    last = table(order, z, size - 1) * cores + other
    count = token_count - rows
    first_tiles([last])
    for c in range(CHUNKS - 1):
        cross_arrival(size - 1, c)
    last_x = pltpu.make_async_copy(
        xg.at[last, pl.ds(0, count)], xv.at[0, pl.ds(0, count)], x_sem.at[0]
    )
    last_x.start()
    last_x.wait()

    def acc_copy(j):
        where = pl.ds(pl.multiple_of(j * cols, cols), cols)
        return pltpu.make_async_copy(
            acc.at[:, :, where], acc_out.at[:, :, where], o_sem.at[4 + j]
        )

    def last_round(j, carry):
        multiply([last], j, count, False)
        acc_copy(j).start()
        return carry

    lax.fori_loop(0, blocks, last_round, 0)

    here(own, shrunk.at[me], 3).wait()
    for k in range(1, n):
        s2_copy(k).wait_recv()
    for k in range(1, groups):
        u2_copy(k).wait_recv()
    for k in range(1, groups):
        d0_copy(k).wait_send()
        d2_copy(k).wait_send()
        u2_copy(k).wait_send()
    for k in range(1, n):
        d1_copy(k).wait_send()
        u1_copy(k).wait_send()
        s1_copy(k).wait_send()
        s2_copy(k).wait_send()

    def drain(i, carry):
        t, c = i // CHUNKS, lax.rem(i, CHUNKS)
        s, across = t * cores + y, t * cores + other

        def sent(s, sems, dev):
            hop(xg.at[s, span(c)], s, c, sems, dev).wait_send()

        @pl.when((z + 1 < size) & (t <= z))
        def _():
            sent(s, up_sem, up_dev)

        @pl.when((z >= 1) & (t >= z))
        def _():
            sent(s, dn_sem, dn_dev)

        near = (t == z - 1) | (t == z + 1)

        @pl.when(jnp.logical_not(near & shifted(size, t, z, c)))
        def _():
            sent(s, y_sem, y_dev)

        @pl.when((t == z) & (z + 1 < size) & shifted(size, z, z + 1, c))
        def _():
            sent(across, up_sem, up_dev)

        @pl.when((t == z) & (z >= 1) & shifted(size, z, z - 1, c))
        def _():
            sent(across, dn_sem, dn_dev)

        return carry

    lax.fori_loop(0, size * CHUNKS, drain, 0)

    def acc_done(j, carry):
        acc_copy(j).wait()
        return carry

    lax.fori_loop(0, blocks, acc_done, 0)
    cross_arrival(size - 1, CHUNKS - 1)


def gather_matmul(tile_rows, tokens, weight, down, up, groups, n):
    token_count, depth = tokens.shape
    hidden = weight.shape[2]
    cols = min(BLOCK_COLS, hidden)
    twice_rank = down.shape[-1]
    share = token_count // n
    dma = pltpu.SemaphoreType.DMA
    any_space = pl.BlockSpec(memory_space=pl.ANY)
    return pl.pallas_call(
        gather_kernel,
        out_shape=(
            jax.ShapeDtypeStruct((n, token_count, depth), tokens.dtype),
            jax.ShapeDtypeStruct((groups,) + up.shape, up.dtype),
            jax.ShapeDtypeStruct((n, share, twice_rank), jnp.bfloat16),
            jax.ShapeDtypeStruct((2, token_count, hidden), jnp.float32),
        ),
        in_specs=[pl.BlockSpec(memory_space=pltpu.SMEM)] + [any_space] * 4,
        out_specs=(any_space,) * 4,
        scratch_shapes=[
            pltpu.VMEM((2, token_count, hidden), jnp.float32),
            pltpu.VMEM((2, token_count, depth), tokens.dtype),
            pltpu.VMEM((2, 2, depth, 2, cols), weight.dtype),
            pltpu.VMEM((groups, n // groups) + down.shape[2:], down.dtype),
            pltpu.VMEM((groups, n) + down.shape[2:], down.dtype),
            pltpu.VMEM((token_count, twice_rank), jnp.bfloat16),
            pltpu.VMEM((n, share, twice_rank), jnp.bfloat16),
            pltpu.VMEM((share, twice_rank), jnp.bfloat16),
            dma((n, CHUNKS)),
            dma((n, CHUNKS)),
            dma((n, CHUNKS)),
            dma((n, CHUNKS)),
            dma((2,)),
            dma((2, 2)),
            dma((groups,)),
            dma((groups,)),
            dma((n,)),
            dma((n,)),
            dma((groups,)),
            dma((groups,)),
            dma((n,)),
            dma((n,)),
            dma((groups,)),
            dma((groups,)),
            dma((n,)),
            dma((n,)),
            dma((n,)),
            dma((n,)),
            dma((4 + hidden // cols,)),
        ],
        compiler_params=pltpu.CompilerParams(
            vmem_limit_bytes=VMEM_LIMIT, has_side_effects=True
        ),
        name="gather_matmul",
    )(tile_rows, tokens, weight, down, up)


def finish_kernel(rank, last_ref, tile_rows, x, w, acc, shrunk, b, out):
    token_count, narrow = out.shape
    rows = x.shape[1]
    start = token_count - rows
    w = jnp.swapaxes(w[...], 0, 1)
    tail = [
        acc[h, start:] + jnp.dot(x[0], w[h], preferred_element_type=jnp.float32)
        for h in range(2)
    ]
    for t in range(token_count // TILE):
        q = tile_rows[t]
        span = slice(t * TILE, (t + 1) * TILE)
        both = []
        for h in range(2):
            delta = jnp.dot(
                shrunk[span, h * rank : (h + 1) * rank],
                b[0, q, :, h * narrow : (h + 1) * narrow],
                preferred_element_type=jnp.float32,
            )
            if t * TILE >= start:
                total = tail[h][t * TILE - start : (t + 1) * TILE - start]
            else:
                total = acc[h, span]
            both.append(total + adapter_scale * delta)
        gate, lift = both
        out[span] = (gate / (1.0 + jnp.exp(-gate)) * lift).astype(out.dtype)


def finish(last, tile_rows, xg, weight, acc, shrunk, u_all):
    _, token_count, depth = xg.shape
    hidden = weight.shape[2]
    groups, pool, rank, twice = u_all.shape
    narrow = twice // 2
    rows = token_count // CHUNKS
    return pl.pallas_call(
        functools.partial(finish_kernel, rank),
        out_shape=jax.ShapeDtypeStruct((token_count, hidden), jnp.bfloat16),
        grid_spec=pltpu.PrefetchScalarGridSpec(
            num_scalar_prefetch=2,
            grid=(groups,),
            in_specs=[
                pl.BlockSpec((1, rows, depth), lambda j, s, q: (s[0], CHUNKS - 1, 0)),
                pl.BlockSpec((depth, 2, narrow), lambda j, s, q: (s[0], 0, j)),
                pl.BlockSpec((2, token_count, narrow), lambda j, s, q: (0, 0, j)),
                pl.BlockSpec((token_count, 2 * rank), lambda j, s, q: (0, 0)),
                pl.BlockSpec((1, pool, rank, twice), lambda j, s, q: (j, 0, 0, 0)),
            ],
            out_specs=pl.BlockSpec((token_count, narrow), lambda j, s, q: (0, j)),
        ),
        compiler_params=pltpu.CompilerParams(vmem_limit_bytes=VMEM_LIMIT),
        name="finish",
    )(last, tile_rows, xg, weight, acc, shrunk, u_all)


def compute_fused(
    tokens,
    gate_up_weight,
    down_factor_pool,
    up_factor_pool,
    segment_adapters,
    segment_tile_counts,
    adapter_pool_rows,
):
    groups = lax.axis_size("grp")
    tp_size, cores_size = lax.axis_size("tp"), lax.axis_size("cores")
    n = tp_size * cores_size
    token_count, depth = tokens.shape
    twice_rank = down_factor_pool.shape[2]
    g, z, y = lax.axis_index("grp"), lax.axis_index("tp"), lax.axis_index("cores")
    tile_count = token_count // TILE
    tile_seg = tile_segments(segment_tile_counts[0], tile_count)
    mine = lax.dynamic_index_in_dim(segment_adapters, g, 0, keepdims=False)
    tile_adapter = jnp.take(mine, tile_seg, mode="clip")
    tile_rows = jnp.take(adapter_pool_rows, tile_adapter, mode="clip").astype(jnp.int32)
    down = down_factor_pool.reshape(n // groups, groups, depth // groups, twice_rank)
    up = up_factor_pool.reshape(up_factor_pool.shape[2:])
    xg, u_all, shrunk, acc = gather_matmul(
        tile_rows, tokens, gate_up_weight, down, up, groups, n
    )
    far = jnp.asarray([row[-1] for row in reach(tp_size)], jnp.int32)[z]
    last = (far * cores_size + (1 - y)).astype(jnp.int32)[None]
    return finish(
        last,
        tile_rows,
        xg,
        gate_up_weight,
        acc,
        shrunk.reshape(token_count, twice_rank),
        u_all,
    )


def fits(mesh):
    size, cores, groups = mesh.shape["tp"], mesh.shape["cores"], mesh.shape["grp"]
    return cores == 2 and 3 <= size <= 4 and (size * cores) % groups == 0


def per_device(*args):
    return compute(*args)


def compute(
    tokens,
    gate_up_weight,
    down_factor_pool,
    up_factor_pool,
    segment_adapters,
    segment_tile_counts,
    adapter_pool_rows,
):
    groups = lax.axis_size("grp")
    tp_size, cores_size = lax.axis_size("tp"), lax.axis_size("cores")
    n = tp_size * cores_size
    token_count, depth = tokens.shape
    local_hidden_width = gate_up_weight.shape[2]
    twice_rank = down_factor_pool.shape[2]
    narrow = local_hidden_width // groups
    seg_count = segment_adapters.shape[1]
    half = token_count // 2

    me = ring_position(lax.axis_index("tp"), lax.axis_index("cores"), tp_size)
    order = [ring_device(k, tp_size, cores_size) for k in range(n)]
    forward = [(order[k], order[(k + 1) % n]) for k in range(n)]
    backward = [(order[(k + 1) % n], order[k]) for k in range(n)]

    def owner(shift):
        return ring_device((me + shift + n) % n, tp_size, cores_size).astype(jnp.int32)

    full_steps = (n - 1) // 2
    lefts, rights = [tokens], [tokens]
    for _ in range(1, full_steps + 1):
        lefts.append(lax.ppermute(lefts[-1], TP, forward))
        rights.append(lax.ppermute(rights[-1], TP, backward))
    last_top = lax.ppermute(lefts[-1][:half], TP, forward)
    last_bottom = lax.ppermute(rights[-1][half:], TP, backward)

    piece = depth // groups
    a = down_factor_pool.reshape(n // groups, groups, piece, twice_rank)
    a = lax.all_to_all(a, "grp", split_axis=1, concat_axis=0, tiled=True)
    a = a.reshape(n, piece, twice_rank)
    a = lax.all_to_all(a, TP, split_axis=0, concat_axis=0, tiled=True)
    b = up_factor_pool.reshape(up_factor_pool.shape[2:])
    b = lax.all_to_all(b, TP, split_axis=0, concat_axis=0, tiled=True)
    slots = jnp.take(adapter_pool_rows, segment_adapters, mode="clip")
    a = group_exchange(a, slots)
    b = group_exchange(b, slots)
    block_cols = narrow
    if narrow % 128:
        block_cols = local_hidden_width
        b = b.reshape(groups, seg_count, b.shape[2], 2, narrow)
        b = jnp.transpose(b, (1, 2, 3, 0, 4))
        b = b.reshape(1, seg_count, b.shape[1], 2 * block_cols)

    tile_count = token_count // TILE
    tile_seg = tile_segments(segment_tile_counts[0], tile_count).astype(jnp.int32)
    row_seg = jnp.repeat(tile_seg, TILE)[:, None]
    partial = None
    for j in range(seg_count):
        term = jnp.dot(
            tokens, a[:, j].reshape(depth, twice_rank), preferred_element_type=jnp.float32
        )
        partial = term if partial is None else jnp.where(row_seg == j, term, partial)
    share = token_count // n
    partial = lax.all_to_all(
        partial.reshape(n, share, twice_rank), TP, split_axis=0, concat_axis=0, tiled=True
    )
    own = jnp.sum(partial, axis=0).astype(jnp.bfloat16)
    shrunk = lax.all_to_all(
        jnp.broadcast_to(own[None], (n, share, twice_rank)),
        TP,
        split_axis=0,
        concat_axis=0,
        tiled=True,
    ).reshape(token_count, twice_rank)

    acc = None
    for s in range(1, full_steps + 1):
        xs = [lefts[s], rights[s]]
        rows = [owner(-s), owner(s)]
        if s == 1:
            xs.insert(0, tokens)
            rows.insert(0, owner(0))
        acc = partial_matmul(xs, gate_up_weight, jnp.stack(rows), acc, block_cols)
    return final_matmul(
        last_top, last_bottom, gate_up_weight, jnp.stack([owner(n // 2)]), acc, shrunk, b, tile_seg
    )


def fused(*args):
    return compute_fused(*args)


def solution(mesh):
    direct = fits(mesh)
    return jax.shard_map(
        fused if direct else per_device,
        mesh=mesh,
        in_specs=(
            P("grp", ("tp", "cores")),
            P(None, None, ("tp", "cores")),
            P(("tp", "cores"), "grp", None),
            P(("tp", "cores"), "grp", None, None, None),
            P(),
            P("grp", None),
            P(),
        ),
        out_specs=P("grp", ("tp", "cores")),
        check_vma=False,
    )
```

profile of v0, /device:TPU:0, one launch (start us, length us, event | category | flops | bytes accessed | tf_op | source)
XLA Modules:
  0.0 283.6 jit_solution(4083386539205793959)
XLA Ops:
  0.0 0.0 copy-start
  0.0 0.7 copy-done
  0.7 1.2 dynamic_slice.7
  2.6 0.8 reduce-window.8
  3.4 0.1 convert_reduce_fusion
  3.5 0.6 gather_fusion
  4.2 1.9 gather_fusion.1
  6.0 259.9 %gather_matmul.1 = (bf16[8,1024,1024]{2,1,0:T(8,128)(2,1)}, bf16[4,8,128,1024]{3,2,1,0:T(8,128)(2,1)}, bf16[8,128,256]{2,1,0:T(8,128)(2,1)}, f32[2,1024,2048]{2,1,0:T(8,128)}) custom-call(s32[8]{0:T(128)} %gather_fusion.1, bf16[1024,1024]{1,0:T(8,128)(2,1)} %tokens.1, bf16[8192,2,2048]{2,1,0:T(2,128)(2,1)} %w.1, bf16[2,4,256,256]{3,2,1,0:T(8,128)(2,1)} %bitcast.10, ...), custom_call_target="tpu_custom_call" | custom-call | tf_op jit(solution)/shard_map/gather_matmul/pallas_call | solution.py:608
  265.9 17.7 %finish.1 = bf16[1024,2048]{1,0:T(8,128)(2,1)} custom-call(s32[1]{0:T(128)} %bitcast.1.last_ref, s32[8]{0:T(128)} %gather_fusion.1, bf16[8,1024,1024]{2,1,0:T(8,128)(2,1)} %get-tuple-element.9.x, bf16[8192,2,2048]{2,1,0:T(2,128)(2,1)} %w.1, f32[2,1024,2048]{2,1,0:T(8,128)} %get-tuple-element.10.acc, bf16[1024,256]{1,0:T(8,128)(2,1)} %bitcast.11, ...), custom_call_target="tpu_custom_call" | custom-call | tf_op jit(solution)/shard_map/finish/pallas_call | solution.py:690
  (3 shorter events, 0.0 us)
Async XLA Ops:
  0.0 0.7 copy-start
where the time goes:
time: 286 us; the launch traced here: 284 us
  Pallas kernels  278 us (97%)
  local copies, waits for them, and re-layouts  4.44 us (2%)
    pallas_call x1, Pallas kernels, gather_matmul(): pl.pallas_call(gather_kernel, out_shape=(jax.ShapeDtypeStruct((n, token_c...  260 us
    pallas_call x1, Pallas kernels, finish(): pl.pallas_call(functools.partial(finish_kernel, rank), out_shape=jax.Shap...  17.7 us

commit v1 on v0

v1 whole, which is shorter than its diff:
```python
import functools

import jax
import jax.numpy as jnp
from jax import lax
from jax.experimental import pallas as pl
from jax.experimental.pallas import tpu as pltpu
from jax.sharding import PartitionSpec as P


TILE = 128
VMEM_LIMIT = 60 * 1024 * 1024

adapter_scale = 0.5


TP = ("tp", "cores")


def tile_segments(tile_lengths, tile_count):
    bounds = jnp.cumsum(tile_lengths)
    positions = jnp.arange(tile_count, dtype=jnp.int32)
    return jnp.sum((bounds[None, :] <= positions[:, None]).astype(jnp.int32), axis=1)


def ring_device(position, tp_size, cores_size):
    c = position // tp_size
    t = position % tp_size
    t = t + (c % 2) * (tp_size - 1 - 2 * t)
    return t * cores_size + c


def ring_position(tp_index, cores_index, tp_size):
    t = tp_index + (cores_index % 2) * (tp_size - 1 - 2 * tp_index)
    return cores_index * tp_size + t


def partial_kernel(count, with_acc, rows_ref, *refs):
    xs, ws = refs[:count], refs[count : 2 * count]
    out = refs[-1]
    ws = [jnp.swapaxes(w[...], 0, 1) for w in ws]
    for h in range(2):
        total = refs[2 * count][h] if with_acc else None
        for x, w in zip(xs, ws):
            term = jnp.dot(x[...], w[h], preferred_element_type=jnp.float32)
            total = term if total is None else total + term
        out[h] = total


def partial_matmul(xs, weight, rows, acc, block_cols):
    count = len(xs)
    tokens, depth = xs[0].shape
    hidden = weight.shape[2]
    block_cols = min(block_cols, 256)
    in_specs = [pl.BlockSpec((tokens, depth), lambda j, r: (0, 0))] * count
    for k in range(count):
        in_specs.append(
            pl.BlockSpec((depth, 2, block_cols), lambda j, r, k=k: (r[k], 0, j))
        )
    acc_spec = pl.BlockSpec((2, tokens, block_cols), lambda j, r: (0, 0, j))
    operands = list(xs) + [weight] * count
    aliases = {}
    if acc is not None:
        in_specs.append(acc_spec)
        aliases = {1 + len(operands): 0}
        operands.append(acc)
    return pl.pallas_call(
        functools.partial(partial_kernel, count, acc is not None),
        out_shape=jax.ShapeDtypeStruct((2, tokens, hidden), jnp.float32),
        grid_spec=pltpu.PrefetchScalarGridSpec(
            num_scalar_prefetch=1,
            grid=(hidden // block_cols,),
            in_specs=in_specs,
            out_specs=acc_spec,
        ),
        input_output_aliases=aliases,
        compiler_params=pltpu.CompilerParams(vmem_limit_bytes=VMEM_LIMIT),
        cost_estimate=pl.CostEstimate(
            flops=4 * count * tokens * depth * hidden,
            bytes_accessed=count * 4 * depth * hidden + 16 * tokens * hidden,
            transcendentals=0,
        ),
    )(rows, *operands)


def final_kernel(tiles_per_half, rank, rows_ref, seg_ref, xt, xb, w, acc, shrunk, b, out, total):
    narrow = out.shape[1]
    w = jnp.swapaxes(w[...], 0, 1)
    for p, x in enumerate((xt, xb)):
        for h in range(2):
            span = slice(p * x.shape[0], (p + 1) * x.shape[0])
            total[h, span] = acc[h, span] + jnp.dot(
                x[...], w[h], preferred_element_type=jnp.float32
            )
        for t in range(p * tiles_per_half, (p + 1) * tiles_per_half):
            seg = seg_ref[t]
            span = slice(t * TILE, (t + 1) * TILE)
            both = []
            for h in range(2):
                delta = jnp.dot(
                    shrunk[span, h * rank : (h + 1) * rank],
                    b[0, seg, :, h * narrow : (h + 1) * narrow],
                    preferred_element_type=jnp.float32,
                )
                both.append(total[h, span] + adapter_scale * delta)
            gate, up = both
            out[span] = (gate / (1.0 + jnp.exp(-gate)) * up).astype(out.dtype)


def final_matmul(xt, xb, weight, rows, acc, shrunk, b_chosen, tile_seg):
    half, depth = xt.shape
    tokens = 2 * half
    hidden = weight.shape[2]
    blocks, segs, rank, twice = b_chosen.shape
    narrow = twice // 2
    return pl.pallas_call(
        functools.partial(final_kernel, half // TILE, rank),
        out_shape=jax.ShapeDtypeStruct((tokens, hidden), jnp.bfloat16),
        grid_spec=pltpu.PrefetchScalarGridSpec(
            num_scalar_prefetch=2,
            grid=(blocks,),
            in_specs=[
                pl.BlockSpec((half, depth), lambda j, r, s: (0, 0)),
                pl.BlockSpec((half, depth), lambda j, r, s: (0, 0)),
                pl.BlockSpec((depth, 2, narrow), lambda j, r, s: (r[0], 0, j)),
                pl.BlockSpec((2, tokens, narrow), lambda j, r, s: (0, 0, j)),
                pl.BlockSpec((tokens, 2 * rank), lambda j, r, s: (0, 0)),
                pl.BlockSpec((1, segs, rank, twice), lambda j, r, s: (j, 0, 0, 0)),
            ],
            out_specs=pl.BlockSpec((tokens, narrow), lambda j, r, s: (0, j)),
            scratch_shapes=[pltpu.VMEM((2, tokens, narrow), jnp.float32)],
        ),
        compiler_params=pltpu.CompilerParams(vmem_limit_bytes=VMEM_LIMIT),
        cost_estimate=pl.CostEstimate(
            flops=4 * tokens * (depth + rank) * hidden,
            bytes_accessed=4 * depth * hidden + 10 * tokens * hidden,
            transcendentals=tokens * hidden,
        ),
    )(rows, tile_seg, xt, xb, weight, acc, shrunk, b_chosen)


def group_exchange(pool, slots):
    groups = lax.axis_size("grp")
    g = lax.axis_index("grp")
    parts = []
    for k in range(groups):
        wanted = lax.dynamic_index_in_dim(slots, (g + k) % groups, 0, keepdims=False)
        part = jnp.take(pool, wanted, axis=0, mode="clip")
        if k:
            pairs = [(i, (i + k) % groups) for i in range(groups)]
            part = lax.ppermute(part, "grp", pairs)
        parts.append(part)
    sources = (g + groups - jnp.arange(groups)) % groups
    return jnp.take(jnp.stack(parts), sources, axis=0, mode="clip")


MESH = pl.DeviceIdType.MESH
CHUNKS = 4
END_SHIFT = 0
BLOCK_COLS = 256


def table(rows, i, k):
    total = 0
    for a, row in enumerate(rows):
        for b, value in enumerate(row):
            if value:
                total = total + jnp.where((i == a) & (k == b), value, 0)
    return total


def reach(size):
    return [sorted(range(size), key=lambda t, z=z: (abs(t - z), t)) for z in range(size)]


def shifted(size, source, dest, c):
    to_end = ((dest == 0) | (dest == size - 1)) & (c >= CHUNKS - END_SHIFT)
    from_end = (source == 0) | (source == size - 1)
    return to_end | from_end


def fused_kernel(
    counts,
    adapters,
    pool_rows,
    tokens,
    weight,
    down,
    up,
    xg,
    out,
    acc,
    xv,
    wbuf,
    d0,
    d1,
    d_pick,
    d_all,
    d_relay,
    u1,
    u_pick,
    u_all,
    u_relay,
    part,
    s_in,
    s_mid,
    s_row,
    shrunk,
    stage,
    recv,
    up_sem,
    dn_sem,
    y_sem,
    x_sem,
    w_sem,
    d0_sem,
    d1_sem,
    d2_sem,
    dr_sem,
    u1_sem,
    u2_sem,
    ur_sem,
    s_sem,
    row_sem,
    g_sem,
    o_sem,
):
    groups = lax.axis_size("grp")
    size, cores = lax.axis_size("tp"), lax.axis_size("cores")
    n = size * cores
    g, z, y = lax.axis_index("grp"), lax.axis_index("tp"), lax.axis_index("cores")
    me = z * cores + y
    other = 1 - y
    token_count, depth = tokens.shape
    rows = token_count // CHUNKS
    hidden = weight.shape[2]
    cols = wbuf.shape[-1]
    blocks = hidden // cols
    per = n // groups
    share = token_count // n
    order = reach(size)
    seg_count = adapters.shape[1]
    rank = up.shape[1]
    narrow = up.shape[2] // 2

    ends = []
    for k in range(seg_count):
        ends.append(counts[0, k] + (ends[-1] if ends else 0))
    tile_seg = []
    for t in range(token_count // TILE):
        seg = 0
        for k in range(seg_count - 1):
            seg = seg + jnp.where(ends[k] <= t, 1, 0)
        tile_seg.append(seg)

    def peer(k):
        return {"grp": lax.rem(g + k, groups)}

    def span(c):
        if isinstance(c, int):
            return pl.ds(c * rows, rows)
        return pl.ds(pl.multiple_of(c * rows, rows), rows)

    def remote(src, dst, send, receive, dev):
        return pltpu.make_async_remote_copy(
            src_ref=src,
            dst_ref=dst,
            send_sem=send,
            recv_sem=receive,
            device_id=dev,
            device_id_type=MESH,
        )


    def hop(src, s, c, sems, dev):
        return remote(src, xg.at[s, span(c)], sems.at[s, c], recv.at[s, c], dev)

    up_dev, dn_dev, y_dev = {"tp": z + 1}, {"tp": z - 1}, {"cores": other}

    def arrived(s, c):
        hop(xg.at[s, span(c)], s, c, y_sem, y_dev).wait_recv()

    def forward(s, c, sems, dev):
        hop(xg.at[s, span(c)], s, c, sems, dev).start()

    def send_own(c):
        src = tokens.at[span(c)]

        @pl.when(z + 1 < size)
        def _():
            hop(src, me, c, up_sem, up_dev).start()

        @pl.when(z >= 1)
        def _():
            hop(src, me, c, dn_sem, dn_dev).start()

        hop(src, me, c, y_sem, y_dev).start()

    def row_arrival(r, c, first):
        lo, hi = z - r, z + r

        @pl.when(lo >= 0)
        def _():
            s = lo * cores + y
            arrived(s, c)

            @pl.when(z + 1 < size)
            def _():
                forward(s, c, up_sem, up_dev)

            @pl.when(jnp.logical_not(shifted(size, lo, z, c)) if first else z >= 0)
            def _():
                forward(s, c, y_sem, y_dev)

        @pl.when(hi < size)
        def _():
            s = hi * cores + y
            arrived(s, c)

            @pl.when(z >= 1)
            def _():
                forward(s, c, dn_sem, dn_dev)

            @pl.when(jnp.logical_not(shifted(size, hi, z, c)) if first else z >= 0)
            def _():
                forward(s, c, y_sem, y_dev)

    def mate_arrival(c):
        s = z * cores + other
        arrived(s, c)

        @pl.when((z + 1 < size) & shifted(size, z, z + 1, c))
        def _():
            forward(s, c, up_sem, up_dev)

        @pl.when((z >= 1) & shifted(size, z, z - 1, c))
        def _():
            forward(s, c, dn_sem, dn_dev)


    def w_copy(piece, j, slot, k):
        return pltpu.make_async_copy(
            weight.at[
                pl.ds(pl.multiple_of(piece * depth, depth), depth),
                slice(None),
                pl.ds(pl.multiple_of(j * cols, cols), cols),
            ],
            wbuf.at[slot, k],
            w_sem.at[slot, k],
        )

    def first_tiles(pieces):
        for k, piece in enumerate(pieces):
            w_copy(piece, 0, 0, k).start()

    def x_copy(src, k):
        return pltpu.make_async_copy(src, xv.at[k], x_sem.at[k])

    def tile_product(pieces, slots, j, where, first):
        slot = lax.rem(j, 2)

        @pl.when(j + 1 < blocks)
        def _():
            for k, piece in enumerate(pieces):
                w_copy(piece, j + 1, 1 - slot, k).start()

        at = pl.ds(pl.multiple_of(j * cols, cols), cols)
        for k, piece in enumerate(pieces):
            w_copy(piece, j, slot, k).wait()
        ws = [jnp.swapaxes(wbuf[slot, k], 0, 1) for k in range(len(pieces))]
        totals = []
        for h in range(2):
            total = None if first else acc[h, where, at]
            for k, x in enumerate(slots):
                term = jnp.dot(xv[x, where], ws[k][h], preferred_element_type=jnp.float32)
                total = term if total is None else total + term
            totals.append(total)
        return at, totals

    def multiply(pieces, slots, j, first):
        at, totals = tile_product(pieces, slots, j, pl.ds(0, token_count), first)
        for h in range(2):
            acc[h, :, at] = totals[h]


    near_end = (z == 1) | (z == size - 2)
    end = jnp.where(z == 1, 0, size - 1)

    def relayed(p_z, p_y, s_z, s_y):
        return ((p_z == 0) | (p_z == size - 1)) & (p_y != s_y) & (p_z != s_z)

    def relay_dev(p_z, p_y):
        return {"tp": jnp.where(p_z == 0, 1, size - 2), "cores": p_y}

    def scatter(source, final, relay, sems, relay_sems, act):
        for k in range(1, n):
            p = lax.rem(me + k, n)
            p_z, p_y = p // cores, lax.rem(p, cores)
            far = relayed(p_z, p_y, z, y)

            @pl.when(far)
            def _():
                copy = remote(
                    source(p), relay.at[z], sems.at[0, p], relay_sems.at[0, z],
                    relay_dev(p_z, p_y),
                )
                act(copy)

            @pl.when(jnp.logical_not(far))
            def _():
                copy = remote(
                    source(p), final.at[me], sems.at[0, p], sems.at[1, me],
                    {"tp": p_z, "cores": p_y},
                )
                act(copy)

    def relay_copy(final, relay, sems, relay_sems, k):
        s_z = lax.rem(end + k, size)
        s = s_z * cores + other
        return s_z, remote(
            relay.at[s_z], final.at[s], relay_sems.at[1, s_z], sems.at[1, s], {"tp": end}
        )

    def pass_on(final, relay, sems, relay_sems):
        @pl.when(near_end)
        def _():
            for k in range(1, size):
                s_z, copy = relay_copy(final, relay, sems, relay_sems, k)
                remote(
                    relay.at[s_z], relay.at[s_z], relay_sems.at[1, s_z], relay_sems.at[0, s_z],
                    {"tp": end},
                ).wait_recv()
                copy.start()

    def scattered(final, sems):
        for k in range(1, n):
            s = lax.rem(me + k, n)
            remote(final.at[s], final.at[s], sems.at[0, s], sems.at[1, s], y_dev).wait_recv()

    def relays_done(final, relay, sems, relay_sems):
        @pl.when(near_end)
        def _():
            for k in range(1, size):
                relay_copy(final, relay, sems, relay_sems, k)[1].wait_send()

    def started(copy):
        copy.start()

    def sent(copy):
        copy.wait_send()

    def d_source(p):
        return d0.at[p // per, lax.rem(p, per)]

    def u_source(p):
        return up.at[p]

    def d_scatter(act):
        scatter(d_source, d1, d_relay, d1_sem, dr_sem, act)

    def u_scatter(act):
        scatter(u_source, u1, u_relay, u1_sem, ur_sem, act)

    def d0_copy(k):
        return remote(
            down.at[:, lax.rem(g + k, groups)], d0.at[g], d0_sem.at[0, k], d0_sem.at[1, k], peer(k)
        )

    def d2_copy(k):
        return remote(d_pick.at[k], d_all.at[g], d2_sem.at[0, k], d2_sem.at[1, k], peer(k))

    def u2_copy(k):
        return remote(u_pick.at[k], u_all.at[g], u2_sem.at[0, k], u2_sem.at[1, k], peer(k))

    def pick(source, picked, mine):
        for k in range(groups):
            which = lax.rem(g + k, groups)
            for j in range(seg_count):
                value = source[pool_rows[adapters[which, j]]]
                if k:
                    picked[k, j] = value
                else:
                    mine[g, j] = value


    def sy_copy():
        return remote(part.at[:, other], s_in, s_sem.at[0], s_sem.at[1], y_dev)

    def sz_copy(k):
        p = lax.rem(z + k, size)
        return remote(s_mid.at[p], s_row.at[k], row_sem.at[0, k], row_sem.at[1, k], {"tp": p})

    def gz_copy(k):
        p = lax.rem(z + k, size)
        return remote(
            shrunk.at[z, y], shrunk.at[z, y], g_sem.at[0, k], g_sem.at[1, k], {"tp": p}
        )

    def gy_copy():
        return remote(shrunk.at[:, y], shrunk.at[:, y], s_sem.at[2], s_sem.at[3], y_dev)

    def shrink():
        piece = depth // groups
        for t in range(token_count // TILE):
            at = slice(t * TILE, (t + 1) * TILE)
            total = None
            for j in range(groups):
                term = jnp.dot(
                    xv[2, at, j * piece : (j + 1) * piece],
                    d_all[j, tile_seg[t]],
                    preferred_element_type=jnp.float32,
                )
                total = term if total is None else total + term
            for i in range(max(1, TILE // share)):
                p = (t * TILE) // share + i
                low = (t * TILE) % share
                length = min(share, TILE)
                part[p // cores, p % cores, low : low + length] = total[
                    i * length : (i + 1) * length
                ]

    def here(src, dst, k):
        return pltpu.make_async_copy(src, dst, o_sem.at[k])


    for k in range(1, groups):
        d0_copy(k).start()
    here(down.at[:, g], d0.at[g], 0).start()
    x_copy(tokens, 2).start()
    first_tiles([me])
    send_own(0)
    here(up.at[me], u1.at[me], 2).start()
    here(down.at[:, g], d0.at[g], 0).wait()
    for k in range(1, groups):
        d0_copy(k).wait_recv()
    d_scatter(started)
    here(d0.at[me // per, lax.rem(me, per)], d1.at[me], 1).start()
    for c in range(1, CHUNKS):
        send_own(c)
    u_scatter(started)
    x_copy(tokens, 2).wait()

    step = blocks // CHUNKS

    def own_tiles(c):
        def one(i, carry):
            multiply([me], [2], c * step + i, True)
            return carry

        lax.fori_loop(0, step, one, 0)

    for c in range(CHUNKS):
        row_arrival(1, c, True)
        mate_arrival(c)
        if c == 1:
            pass_on(d1, d_relay, d1_sem, dr_sem)
        if c == CHUNKS - 1:
            here(d0.at[me // per, lax.rem(me, per)], d1.at[me], 1).wait()
            scattered(d1, d1_sem)
            pick(d1, d_pick, d_all)
            pass_on(u1, u_relay, u1_sem, ur_sem)
            for k in range(1, groups):
                d2_copy(k).start()
        own_tiles(c)

    def later_round(r, carry):
        pieces = [
            table(order, z, r - 1) * cores + y,
            table(order, z, r - 2) * cores + other,
        ]

        @pl.when(r >= 3)
        def _():
            for c in range(CHUNKS):
                arrived(pieces[1], c)

        for k in range(2):
            x_copy(xg.at[pieces[k]], k).start()
        first_tiles(pieces)
        for k in range(2):
            x_copy(xg.at[pieces[k]], k).wait()

        def body(c, carry):
            @pl.when(r < size)
            def _():
                row_arrival(r, c, False)

            @pl.when((r == 2) & (c == 0))
            def _():
                for k in range(1, groups):
                    d2_copy(k).wait_recv()
                shrink()
                here(up.at[me], u1.at[me], 2).wait()
                scattered(u1, u1_sem)
                pick(u1, u_pick, u_all)
                sy_copy().start()

            @pl.when((r == 2) & (c == 1))
            def _():
                for k in range(1, groups):
                    u2_copy(k).start()

            @pl.when((r == 2) & (c == 2))
            def _():
                sy_copy().wait_recv()
                for k in range(size):
                    s_mid[k] = part[k, y] + s_in[k]

            @pl.when((r == 2) & (c == 3))
            def _():
                for k in range(1, size):
                    sz_copy(k).start()

            @pl.when((r == 3) & (c == 0))
            def _():
                mine = s_mid[z]
                for k in range(1, size):
                    sz_copy(k).wait_recv()
                    mine = mine + s_row[k]
                shrunk[z, y] = mine.astype(shrunk.dtype)

            @pl.when((r == 3) & (c == 1))
            def _():
                for k in range(1, size):
                    gz_copy(k).start()

            @pl.when((r == 3) & (c == 2))
            def _():
                for k in range(1, size):
                    p = lax.rem(z + size - k, size)
                    remote(
                        shrunk.at[p, y], shrunk.at[p, y], g_sem.at[0, k], g_sem.at[1, k], y_dev
                    ).wait_recv()
                gy_copy().start()

            def one(i, carry):
                multiply(pieces, [0, 1], c * step + i, False)
                return carry

            lax.fori_loop(0, step, one, 0)
            return carry

        lax.fori_loop(0, CHUNKS, body, 0)
        return carry

    lax.fori_loop(2, size + 1, later_round, 0)


    last = table(order, z, size - 1) * cores + other

    def last_x(c):
        return pltpu.make_async_copy(xg.at[last, span(c)], xv.at[0, span(c)], x_sem.at[0])

    def stage_copy(c):
        return pltpu.make_async_copy(stage.at[c % 2], out.at[span(c)], o_sem.at[4 + c % 2])

    def tail(c):
        def one(j, carry):
            at, totals = tile_product([last], [0], j, span(c), False)
            m = (j * cols) // narrow
            low = lax.rem(j * cols, narrow)
            for t in range(rows // TILE):
                tile = c * (rows // TILE) + t
                both = []
                for h in range(2):
                    parts = []
                    for i in range(max(1, TILE // share)):
                        p = (tile * TILE) // share + i
                        first = (tile * TILE) % share
                        parts.append(
                            shrunk[
                                p // cores,
                                p % cores,
                                first : first + min(share, TILE),
                                h * rank : (h + 1) * rank,
                            ]
                        )
                    x = parts[0] if len(parts) == 1 else jnp.concatenate(parts, 0)
                    delta = jnp.dot(
                        x,
                        u_all[
                            m,
                            tile_seg[tile],
                            :,
                            pl.ds(pl.multiple_of(h * narrow + low, cols), cols),
                        ],
                        preferred_element_type=jnp.float32,
                    )
                    both.append(
                        totals[h][t * TILE : (t + 1) * TILE] + adapter_scale * delta
                    )
                gate, lift = both
                value = gate / (1.0 + jnp.exp(-gate)) * lift
                stage[c % 2, t * TILE : (t + 1) * TILE, at] = value.astype(stage.dtype)
            return carry

        lax.fori_loop(0, blocks, one, 0)

    def drain(i, carry):
        t, c = i // CHUNKS, lax.rem(i, CHUNKS)
        s, across = t * cores + y, t * cores + other

        def done(s, sems, dev):
            hop(xg.at[s, span(c)], s, c, sems, dev).wait_send()

        @pl.when((z + 1 < size) & (t <= z))
        def _():
            done(s, up_sem, up_dev)

        @pl.when((z >= 1) & (t >= z))
        def _():
            done(s, dn_sem, dn_dev)

        near = (t == z - 1) | (t == z + 1)

        @pl.when(jnp.logical_not(near & shifted(size, t, z, c)))
        def _():
            done(s, y_sem, y_dev)

        @pl.when((t == z) & (z + 1 < size) & shifted(size, z, z + 1, c))
        def _():
            done(across, up_sem, up_dev)

        @pl.when((t == z) & (z >= 1) & shifted(size, z, z - 1, c))
        def _():
            done(across, dn_sem, dn_dev)

        return carry

    def all_sent():
        for k in range(1, groups):
            d0_copy(k).wait_send()
            d2_copy(k).wait_send()
            u2_copy(k).wait_send()
        d_scatter(sent)
        u_scatter(sent)
        relays_done(d1, d_relay, d1_sem, dr_sem)
        relays_done(u1, u_relay, u1_sem, ur_sem)
        sy_copy().wait_send()
        gy_copy().wait_send()
        for k in range(1, size):
            sz_copy(k).wait_send()
            gz_copy(k).wait_send()
        lax.fori_loop(0, size * CHUNKS, drain, 0)

    for c in range(CHUNKS):
        first_tiles([last])
        if c == 0:
            for k in range(1, groups):
                u2_copy(k).wait_recv()
            remote(
                shrunk.at[:, other], shrunk.at[:, other], s_sem.at[2], s_sem.at[3], y_dev
            ).wait_recv()
        if c == CHUNKS - 1:
            all_sent()
        arrived(last, c)
        last_x(c).start()
        if c >= 2:
            stage_copy(c - 2).wait()
        last_x(c).wait()
        tail(c)
        stage_copy(c).start()
    for c in range(max(0, CHUNKS - 2), CHUNKS):
        stage_copy(c).wait()


def fused_call(counts, adapters, pool_rows, tokens, weight, down, up, groups, size, cores):
    n = size * cores
    token_count, depth = tokens.shape
    hidden = weight.shape[2]
    cols = min(BLOCK_COLS, hidden)
    twice_rank = down.shape[-1]
    share = token_count // n
    segs = adapters.shape[1]
    dma = pltpu.SemaphoreType.DMA
    any_space = pl.BlockSpec(memory_space=pl.ANY)
    smem = pl.BlockSpec(memory_space=pltpu.SMEM)
    block = down.shape[2:]
    leaf = up.shape[1:]
    vmem = pltpu.VMEM
    return pl.pallas_call(
        fused_kernel,
        out_shape=(
            jax.ShapeDtypeStruct((n, token_count, depth), tokens.dtype),
            jax.ShapeDtypeStruct((token_count, hidden), jnp.bfloat16),
        ),
        in_specs=[smem] * 3 + [any_space] * 4,
        out_specs=(any_space,) * 2,
        scratch_shapes=[
            vmem((2, token_count, hidden), jnp.float32),
            vmem((3, token_count, depth), tokens.dtype),
            vmem((2, 2, depth, 2, cols), weight.dtype),
            vmem((groups, n // groups) + block, down.dtype),
            vmem((n,) + block, down.dtype),
            vmem((groups, segs) + block, down.dtype),
            vmem((groups, segs) + block, down.dtype),
            vmem((size,) + block, down.dtype),
            vmem((n,) + leaf, up.dtype),
            vmem((groups, segs) + leaf, up.dtype),
            vmem((groups, segs) + leaf, up.dtype),
            vmem((size,) + leaf, up.dtype),
            vmem((size, cores, share, twice_rank), jnp.float32),
            vmem((size, share, twice_rank), jnp.float32),
            vmem((size, share, twice_rank), jnp.float32),
            vmem((size, share, twice_rank), jnp.float32),
            vmem((size, cores, share, twice_rank), jnp.bfloat16),
            vmem((2, token_count // CHUNKS, hidden), jnp.bfloat16),
            dma((n, CHUNKS)),
            dma((n, CHUNKS)),
            dma((n, CHUNKS)),
            dma((n, CHUNKS)),
            dma((3,)),
            dma((2, 2)),
            dma((2, groups)),
            dma((2, n)),
            dma((2, groups)),
            dma((2, size)),
            dma((2, n)),
            dma((2, groups)),
            dma((2, size)),
            dma((4,)),
            dma((2, size)),
            dma((2, size)),
            dma((6,)),
        ],
        compiler_params=pltpu.CompilerParams(
            vmem_limit_bytes=VMEM_LIMIT, has_side_effects=True
        ),
        name="fused",
    )(counts, adapters, pool_rows, tokens, weight, down, up)


def compute_fused(
    tokens,
    gate_up_weight,
    down_factor_pool,
    up_factor_pool,
    segment_adapters,
    segment_tile_counts,
    adapter_pool_rows,
):
    groups = lax.axis_size("grp")
    size, cores = lax.axis_size("tp"), lax.axis_size("cores")
    n = size * cores
    depth = tokens.shape[1]
    down = down_factor_pool.reshape(
        n // groups, groups, depth // groups, down_factor_pool.shape[2]
    )
    up = up_factor_pool.reshape(up_factor_pool.shape[2:])
    return fused_call(
        segment_tile_counts,
        segment_adapters,
        adapter_pool_rows,
        tokens,
        gate_up_weight,
        down,
        up,
        groups,
        size,
        cores,
    )[1]


def fits(mesh):
    size, cores, groups = mesh.shape["tp"], mesh.shape["cores"], mesh.shape["grp"]
    return cores == 2 and size == groups and (size * cores) % groups == 0 and size == 4


def per_device(*args):
    return compute(*args)


def compute(
    tokens,
    gate_up_weight,
    down_factor_pool,
    up_factor_pool,
    segment_adapters,
    segment_tile_counts,
    adapter_pool_rows,
):
    groups = lax.axis_size("grp")
    tp_size, cores_size = lax.axis_size("tp"), lax.axis_size("cores")
    n = tp_size * cores_size
    token_count, depth = tokens.shape
    local_hidden_width = gate_up_weight.shape[2]
    twice_rank = down_factor_pool.shape[2]
    narrow = local_hidden_width // groups
    seg_count = segment_adapters.shape[1]
    half = token_count // 2

    me = ring_position(lax.axis_index("tp"), lax.axis_index("cores"), tp_size)
    order = [ring_device(k, tp_size, cores_size) for k in range(n)]
    forward = [(order[k], order[(k + 1) % n]) for k in range(n)]
    backward = [(order[(k + 1) % n], order[k]) for k in range(n)]

    def owner(shift):
        return ring_device((me + shift + n) % n, tp_size, cores_size).astype(jnp.int32)

    full_steps = (n - 1) // 2
    lefts, rights = [tokens], [tokens]
    for _ in range(1, full_steps + 1):
        lefts.append(lax.ppermute(lefts[-1], TP, forward))
        rights.append(lax.ppermute(rights[-1], TP, backward))
    last_top = lax.ppermute(lefts[-1][:half], TP, forward)
    last_bottom = lax.ppermute(rights[-1][half:], TP, backward)

    piece = depth // groups
    a = down_factor_pool.reshape(n // groups, groups, piece, twice_rank)
    a = lax.all_to_all(a, "grp", split_axis=1, concat_axis=0, tiled=True)
    a = a.reshape(n, piece, twice_rank)
    a = lax.all_to_all(a, TP, split_axis=0, concat_axis=0, tiled=True)
    b = up_factor_pool.reshape(up_factor_pool.shape[2:])
    b = lax.all_to_all(b, TP, split_axis=0, concat_axis=0, tiled=True)
    slots = jnp.take(adapter_pool_rows, segment_adapters, mode="clip")
    a = group_exchange(a, slots)
    b = group_exchange(b, slots)
    block_cols = narrow
    if narrow % 128:
        block_cols = local_hidden_width
        b = b.reshape(groups, seg_count, b.shape[2], 2, narrow)
        b = jnp.transpose(b, (1, 2, 3, 0, 4))
        b = b.reshape(1, seg_count, b.shape[1], 2 * block_cols)

    tile_count = token_count // TILE
    tile_seg = tile_segments(segment_tile_counts[0], tile_count).astype(jnp.int32)
    row_seg = jnp.repeat(tile_seg, TILE)[:, None]
    partial = None
    for j in range(seg_count):
        term = jnp.dot(
            tokens, a[:, j].reshape(depth, twice_rank), preferred_element_type=jnp.float32
        )
        partial = term if partial is None else jnp.where(row_seg == j, term, partial)
    share = token_count // n
    partial = lax.all_to_all(
        partial.reshape(n, share, twice_rank), TP, split_axis=0, concat_axis=0, tiled=True
    )
    own = jnp.sum(partial, axis=0).astype(jnp.bfloat16)
    shrunk = lax.all_to_all(
        jnp.broadcast_to(own[None], (n, share, twice_rank)),
        TP,
        split_axis=0,
        concat_axis=0,
        tiled=True,
    ).reshape(token_count, twice_rank)

    acc = None
    for s in range(1, full_steps + 1):
        xs = [lefts[s], rights[s]]
        rows = [owner(-s), owner(s)]
        if s == 1:
            xs.insert(0, tokens)
            rows.insert(0, owner(0))
        acc = partial_matmul(xs, gate_up_weight, jnp.stack(rows), acc, block_cols)
    return final_matmul(
        last_top, last_bottom, gate_up_weight, jnp.stack([owner(n // 2)]), acc, shrunk, b, tile_seg
    )


def fused(*args):
    return compute_fused(*args)


def solution(mesh):
    direct = fits(mesh)
    return jax.shard_map(
        fused if direct else per_device,
        mesh=mesh,
        in_specs=(
            P("grp", ("tp", "cores")),
            P(None, None, ("tp", "cores")),
            P(("tp", "cores"), "grp", None),
            P(("tp", "cores"), "grp", None, None, None),
            P(),
            P("grp", None),
            P(),
        ),
        out_specs=P("grp", ("tp", "cores")),
        check_vma=False,
    )
```

time: 286 us -> 302 us (1.056)
  Pallas kernels: 278 us -> 296 us
    pallas_call x2 -> x1, Pallas kernels: 278 us -> 296 us  [fused_call(): pl.pallas_call(fused_kernel, out_shape=(jax.ShapeDtypeStruct((n, token_co...]
    unnamed x2 -> x1, local copies, waits for them, and re-layouts: 0.68 us -> 4.79 us
where the time goes in v1:
time: 302 us; the launch traced here: 301 us
  Pallas kernels  296 us (98%)
  local copies, waits for them, and re-layouts  4.79 us (2%)
    pallas_call x1, Pallas kernels, fused_call(): pl.pallas_call(fused_kernel, out_shape=(jax.ShapeDtypeStruct((n, token_co...  296 us

profile of v1, /device:TPU:0, one launch (start us, length us, event | category | flops | bytes accessed | tf_op | source)
XLA Modules:
  0.0 301.1 jit_solution(4102012645529540400)
XLA Ops:
  0.0 296.3 %fused.1 = (bf16[8,1024,1024]{2,1,0:T(8,128)(2,1)}, bf16[1024,2048]{1,0:T(8,128)(2,1)}) custom-call(s32[1,3]{1,0:T(1,128)} %counts.1, s32[4,3]{1,0:T(4,128)} %adapters.1, s32[8]{0:T(128)} %pool_rows.1, bf16[1024,1024]{1,0:T(8,128)(2,1)} %tokens.1, bf16[8192,2,2048]{2,1,0:T(2,128)(2,1)} %weight.1, bf16[2,4,256,256]{3,2,1,0:T(8,128)(2,1)} %bitcast.3, ...), custom_call_target="tpu_custom_call" | custom-call | tf_op jit(solution)/shard_map/fused/pallas_call | solution.py:781
  296.3 4.8 %copy.9 = bf16[1024,2048]{1,0:T(8,128)(2,1)} copy(bf16[1024,2048]{1,0:T(8,128)(2,1)} %get-tuple-element.6) | data formatting | bytes 8388608

commit v2 on v1

--- a/solution.py
+++ b/solution.py
@@ -192,19 +192,14 @@
     acc,
     xv,
     wbuf,
-    d0,
-    d1,
-    d_pick,
     d_all,
-    d_relay,
+    low,
     u1,
     u_pick,
     u_all,
     u_relay,
     part,
     s_in,
-    s_mid,
-    s_row,
     shrunk,
     stage,
     recv,
@@ -213,15 +208,11 @@
     y_sem,
     x_sem,
     w_sem,
-    d0_sem,
-    d1_sem,
-    d2_sem,
-    dr_sem,
+    d_sem,
     u1_sem,
     u2_sem,
     ur_sem,
     s_sem,
-    row_sem,
     g_sem,
     o_sem,
 ):
@@ -237,11 +228,11 @@
     cols = wbuf.shape[-1]
     blocks = hidden // cols
     per = n // groups
-    share = token_count // n
     order = reach(size)
     seg_count = adapters.shape[1]
     rank = up.shape[1]
     narrow = up.shape[2] // 2
+    piece_rows = rows // n
 
     ends = []
     for k in range(seg_count):
@@ -283,7 +274,7 @@
     def forward(s, c, sems, dev):
         hop(xg.at[s, span(c)], s, c, sems, dev).start()
 
-    def send_own(c):
+    def send_row(c):
         src = tokens.at[span(c)]
 
         @pl.when(z + 1 < size)
@@ -294,7 +285,8 @@
         def _():
             hop(src, me, c, dn_sem, dn_dev).start()
 
-        hop(src, me, c, y_sem, y_dev).start()
+    def send_mate(c):
+        hop(tokens.at[span(c)], me, c, y_sem, y_dev).start()
 
     def row_arrival(r, c, first):
         lo, hi = z - r, z + r
@@ -356,7 +348,7 @@
     def x_copy(src, k):
         return pltpu.make_async_copy(src, xv.at[k], x_sem.at[k])
 
-    def tile_product(pieces, slots, j, where, first):
+    def multiply(pieces, j, low_row, count, first):
         slot = lax.rem(j, 2)
 
         @pl.when(j + 1 < blocks)
@@ -365,22 +357,37 @@
                 w_copy(piece, j + 1, 1 - slot, k).start()
 
         at = pl.ds(pl.multiple_of(j * cols, cols), cols)
+        where = pl.ds(low_row, count)
         for k, piece in enumerate(pieces):
             w_copy(piece, j, slot, k).wait()
         ws = [jnp.swapaxes(wbuf[slot, k], 0, 1) for k in range(len(pieces))]
-        totals = []
         for h in range(2):
             total = None if first else acc[h, where, at]
-            for k, x in enumerate(slots):
-                term = jnp.dot(xv[x, where], ws[k][h], preferred_element_type=jnp.float32)
+            for k in range(len(pieces)):
+                term = jnp.dot(xv[k, where], ws[k][h], preferred_element_type=jnp.float32)
                 total = term if total is None else total + term
-            totals.append(total)
-        return at, totals
-
-    def multiply(pieces, slots, j, first):
-        at, totals = tile_product(pieces, slots, j, pl.ds(0, token_count), first)
-        for h in range(2):
-            acc[h, :, at] = totals[h]
+            acc[h, where, at] = total
+
+    def run_round(pieces, sources, first=False, project=True, hooks=()):
+        first_tiles(pieces)
+        copies = [x_copy(src, k) for k, src in enumerate(sources)]
+        for copy in copies:
+            copy.start()
+        for copy in copies:
+            copy.wait()
+        if project:
+            for k, piece in enumerate(pieces):
+                low[...] = low[...] + jnp.dot(
+                    xv[k], d_all[piece], preferred_element_type=jnp.float32
+                )
+
+        def one(j, carry):
+            multiply(pieces, j, 0, token_count, first)
+            for i, hook in enumerate(hooks):
+                pl.when(j == (i + 1) * blocks // len(hooks) - 1)(hook)
+            return carry
+
+        lax.fori_loop(0, blocks, one, 0)
 
 
     near_end = (z == 1) | (z == size - 2)
@@ -449,25 +456,15 @@
     def sent(copy):
         copy.wait_send()
 
-    def d_source(p):
-        return d0.at[p // per, lax.rem(p, per)]
-
     def u_source(p):
         return up.at[p]
 
-    def d_scatter(act):
-        scatter(d_source, d1, d_relay, d1_sem, dr_sem, act)
-
     def u_scatter(act):
         scatter(u_source, u1, u_relay, u1_sem, ur_sem, act)
 
-    def d0_copy(k):
-        return remote(
-            down.at[:, lax.rem(g + k, groups)], d0.at[g], d0_sem.at[0, k], d0_sem.at[1, k], peer(k)
-        )
-
-    def d2_copy(k):
-        return remote(d_pick.at[k], d_all.at[g], d2_sem.at[0, k], d2_sem.at[1, k], peer(k))
+    def d_copy(k):
+        mine = d_all.at[pl.ds(g * per, per)]
+        return remote(down, mine, d_sem.at[0, k], d_sem.at[1, k], peer(k))
 
     def u2_copy(k):
         return remote(u_pick.at[k], u_all.at[g], u2_sem.at[0, k], u2_sem.at[1, k], peer(k))
@@ -483,218 +480,92 @@
                     mine[g, j] = value
 
 
-    def sy_copy():
-        return remote(part.at[:, other], s_in, s_sem.at[0], s_sem.at[1], y_dev)
-
-    def sz_copy(k):
-        p = lax.rem(z + k, size)
-        return remote(s_mid.at[p], s_row.at[k], row_sem.at[0, k], row_sem.at[1, k], {"tp": p})
-
-    def gz_copy(k):
-        p = lax.rem(z + k, size)
+    tile_rows = [pool_rows[adapters[g, seg]] for seg in tile_seg]
+
+    def low_send(c):
+        base = c * rows
+        for t in range(rows // TILE):
+            tile = c * (rows // TILE) + t
+            value = low[base + t * TILE : base + (t + 1) * TILE]
+            value = jnp.where(tile_rows[tile] == me, value, 0.0).astype(part.dtype)
+            count = TILE // piece_rows
+            for i in range(count):
+                part[c, t * count + i] = value[i * piece_rows : (i + 1) * piece_rows]
+        for k in range(1, n):
+            s_copy(c, k).start()
+
+    def mate(k):
+        p = lax.rem(me + k, n)
+        return p, {"tp": p // cores, "cores": lax.rem(p, cores)}
+
+    def s_copy(c, k):
+        p, dev = mate(k)
         return remote(
-            shrunk.at[z, y], shrunk.at[z, y], g_sem.at[0, k], g_sem.at[1, k], {"tp": p}
+            part.at[c, p], s_in.at[c, k], s_sem.at[0, c, k], s_sem.at[1, c, k], dev
         )
 
-    def gy_copy():
-        return remote(shrunk.at[:, y], shrunk.at[:, y], s_sem.at[2], s_sem.at[3], y_dev)
-
-    def shrink():
-        piece = depth // groups
-        for t in range(token_count // TILE):
-            at = slice(t * TILE, (t + 1) * TILE)
-            total = None
-            for j in range(groups):
-                term = jnp.dot(
-                    xv[2, at, j * piece : (j + 1) * piece],
-                    d_all[j, tile_seg[t]],
-                    preferred_element_type=jnp.float32,
-                )
-                total = term if total is None else total + term
-            for i in range(max(1, TILE // share)):
-                p = (t * TILE) // share + i
-                low = (t * TILE) % share
-                length = min(share, TILE)
-                part[p // cores, p % cores, low : low + length] = total[
-                    i * length : (i + 1) * length
-                ]
+    def g_copy(c, k):
+        _, dev = mate(k)
+        mine = shrunk.at[c, me]
+        return remote(mine, mine, g_sem.at[0, c, k], g_sem.at[1, c, k], dev)
+
+    def low_sum(c):
+        total = part[c, me].astype(jnp.float32)
+        for k in range(1, n):
+            s_copy(c, k).wait_recv()
+            total = total + s_in[c, k].astype(jnp.float32)
+        shrunk[c, me] = total.astype(shrunk.dtype)
+
+    def low_share(c):
+        for k in range(1, n):
+            g_copy(c, k).start()
+
+    def low_ready(c):
+        for k in range(1, n):
+            p = lax.rem(me + n - k, n)
+            mine = shrunk.at[c, p]
+            remote(mine, mine, g_sem.at[0, c, k], g_sem.at[1, c, k], y_dev).wait_recv()
 
     def here(src, dst, k):
         return pltpu.make_async_copy(src, dst, o_sem.at[k])
 
-
-    for k in range(1, groups):
-        d0_copy(k).start()
-    here(down.at[:, g], d0.at[g], 0).start()
-    x_copy(tokens, 2).start()
-    first_tiles([me])
-    send_own(0)
-    here(up.at[me], u1.at[me], 2).start()
-    here(down.at[:, g], d0.at[g], 0).wait()
-    for k in range(1, groups):
-        d0_copy(k).wait_recv()
-    d_scatter(started)
-    here(d0.at[me // per, lax.rem(me, per)], d1.at[me], 1).start()
-    for c in range(1, CHUNKS):
-        send_own(c)
-    u_scatter(started)
-    x_copy(tokens, 2).wait()
-
-    step = blocks // CHUNKS
-
-    def own_tiles(c):
-        def one(i, carry):
-            multiply([me], [2], c * step + i, True)
-            return carry
-
-        lax.fori_loop(0, step, one, 0)
-
-    for c in range(CHUNKS):
-        row_arrival(1, c, True)
-        mate_arrival(c)
-        if c == 1:
-            pass_on(d1, d_relay, d1_sem, dr_sem)
-        if c == CHUNKS - 1:
-            here(d0.at[me // per, lax.rem(me, per)], d1.at[me], 1).wait()
-            scattered(d1, d1_sem)
-            pick(d1, d_pick, d_all)
-            pass_on(u1, u_relay, u1_sem, ur_sem)
-            for k in range(1, groups):
-                d2_copy(k).start()
-        own_tiles(c)
-
-    def later_round(r, carry):
-        pieces = [
-            table(order, z, r - 1) * cores + y,
-            table(order, z, r - 2) * cores + other,
-        ]
-
-        @pl.when(r >= 3)
-        def _():
-            for c in range(CHUNKS):
-                arrived(pieces[1], c)
-
-        for k in range(2):
-            x_copy(xg.at[pieces[k]], k).start()
-        first_tiles(pieces)
-        for k in range(2):
-            x_copy(xg.at[pieces[k]], k).wait()
-
-        def body(c, carry):
-            @pl.when(r < size)
-            def _():
-                row_arrival(r, c, False)
-
-            @pl.when((r == 2) & (c == 0))
-            def _():
-                for k in range(1, groups):
-                    d2_copy(k).wait_recv()
-                shrink()
-                here(up.at[me], u1.at[me], 2).wait()
-                scattered(u1, u1_sem)
-                pick(u1, u_pick, u_all)
-                sy_copy().start()
-
-            @pl.when((r == 2) & (c == 1))
-            def _():
-                for k in range(1, groups):
-                    u2_copy(k).start()
-
-            @pl.when((r == 2) & (c == 2))
-            def _():
-                sy_copy().wait_recv()
-                for k in range(size):
-                    s_mid[k] = part[k, y] + s_in[k]
-
-            @pl.when((r == 2) & (c == 3))
-            def _():
-                for k in range(1, size):
-                    sz_copy(k).start()
-
-            @pl.when((r == 3) & (c == 0))
-            def _():
-                mine = s_mid[z]
-                for k in range(1, size):
-                    sz_copy(k).wait_recv()
-                    mine = mine + s_row[k]
-                shrunk[z, y] = mine.astype(shrunk.dtype)
-
-            @pl.when((r == 3) & (c == 1))
-            def _():
-                for k in range(1, size):
-                    gz_copy(k).start()
-
-            @pl.when((r == 3) & (c == 2))
-            def _():
-                for k in range(1, size):
-                    p = lax.rem(z + size - k, size)
-                    remote(
-                        shrunk.at[p, y], shrunk.at[p, y], g_sem.at[0, k], g_sem.at[1, k], y_dev
-                    ).wait_recv()
-                gy_copy().start()
-
-            def one(i, carry):
-                multiply(pieces, [0, 1], c * step + i, False)
-                return carry
-
-            lax.fori_loop(0, step, one, 0)
-            return carry
-
-        lax.fori_loop(0, CHUNKS, body, 0)
-        return carry
-
-    lax.fori_loop(2, size + 1, later_round, 0)
-
-
-    last = table(order, z, size - 1) * cores + other
-
-    def last_x(c):
-        return pltpu.make_async_copy(xg.at[last, span(c)], xv.at[0, span(c)], x_sem.at[0])
-
     def stage_copy(c):
         return pltpu.make_async_copy(stage.at[c % 2], out.at[span(c)], o_sem.at[4 + c % 2])
 
-    def tail(c):
+    def epilogue(c):
+        base = c * rows
+        if c >= 2:
+            stage_copy(c - 2).wait()
+
         def one(j, carry):
-            at, totals = tile_product([last], [0], j, span(c), False)
+            at = pl.ds(pl.multiple_of(j * cols, cols), cols)
             m = (j * cols) // narrow
-            low = lax.rem(j * cols, narrow)
+            offset = lax.rem(j * cols, narrow)
             for t in range(rows // TILE):
                 tile = c * (rows // TILE) + t
+                count = TILE // piece_rows
+                x = shrunk[c, t * count : (t + 1) * count].reshape(TILE, 2 * rank)
                 both = []
                 for h in range(2):
-                    parts = []
-                    for i in range(max(1, TILE // share)):
-                        p = (tile * TILE) // share + i
-                        first = (tile * TILE) % share
-                        parts.append(
-                            shrunk[
-                                p // cores,
-                                p % cores,
-                                first : first + min(share, TILE),
-                                h * rank : (h + 1) * rank,
-                            ]
-                        )
-                    x = parts[0] if len(parts) == 1 else jnp.concatenate(parts, 0)
                     delta = jnp.dot(
-                        x,
+                        x[:, h * rank : (h + 1) * rank],
                         u_all[
                             m,
                             tile_seg[tile],
                             :,
-                            pl.ds(pl.multiple_of(h * narrow + low, cols), cols),
+                            pl.ds(pl.multiple_of(h * narrow + offset, cols), cols),
                         ],
                         preferred_element_type=jnp.float32,
                     )
-                    both.append(
-                        totals[h][t * TILE : (t + 1) * TILE] + adapter_scale * delta
-                    )
+                    total = acc[h, base + t * TILE : base + (t + 1) * TILE, at]
+                    both.append(total + adapter_scale * delta)
                 gate, lift = both
                 value = gate / (1.0 + jnp.exp(-gate)) * lift
                 stage[c % 2, t * TILE : (t + 1) * TILE, at] = value.astype(stage.dtype)
             return carry
 
         lax.fori_loop(0, blocks, one, 0)
+        stage_copy(c).start()
 
     def drain(i, carry):
         t, c = i // CHUNKS, lax.rem(i, CHUNKS)
@@ -729,37 +600,118 @@
 
     def all_sent():
         for k in range(1, groups):
-            d0_copy(k).wait_send()
-            d2_copy(k).wait_send()
+            d_copy(k).wait_send()
             u2_copy(k).wait_send()
-        d_scatter(sent)
         u_scatter(sent)
-        relays_done(d1, d_relay, d1_sem, dr_sem)
         relays_done(u1, u_relay, u1_sem, ur_sem)
-        sy_copy().wait_send()
-        gy_copy().wait_send()
-        for k in range(1, size):
-            sz_copy(k).wait_send()
-            gz_copy(k).wait_send()
         lax.fori_loop(0, size * CHUNKS, drain, 0)
 
+    def row_piece(i):
+        return table(order, z, i) * cores + y
+
+    def cross_piece(i):
+        return table(order, z, i) * cores + other
+
+    def near_arrivals(c):
+        row_arrival(1, c, True)
+        mate_arrival(c)
+
+    def cross_ready(piece):
+        for c in range(CHUNKS):
+            arrived(piece, c)
+
+    far = cross_piece(size - 1)
+
+
     for c in range(CHUNKS):
-        first_tiles([last])
-        if c == 0:
-            for k in range(1, groups):
-                u2_copy(k).wait_recv()
-            remote(
-                shrunk.at[:, other], shrunk.at[:, other], s_sem.at[2], s_sem.at[3], y_dev
-            ).wait_recv()
-        if c == CHUNKS - 1:
-            all_sent()
-        arrived(last, c)
-        last_x(c).start()
-        if c >= 2:
-            stage_copy(c - 2).wait()
-        last_x(c).wait()
-        tail(c)
-        stage_copy(c).start()
+        send_row(c)
+        send_mate(c)
+    for k in range(1, groups):
+        d_copy(k).start()
+    here(down, d_all.at[pl.ds(g * per, per)], 0).start()
+    here(up.at[me], u1.at[me], 1).start()
+    u_scatter(started)
+    run_round(
+        [me], [tokens], True, False,
+        [functools.partial(near_arrivals, c) for c in range(CHUNKS)],
+    )
+    here(down, d_all.at[pl.ds(g * per, per)], 0).wait()
+    for k in range(1, groups):
+        d_copy(k).wait_recv()
+    low[...] = jnp.dot(xv[0], d_all[me], preferred_element_type=jnp.float32)
+    pair = [row_piece(1), cross_piece(0)]
+    run_round(pair, [xg.at[q] for q in pair])
+    pass_on(u1, u_relay, u1_sem, ur_sem)
+    row_arrival(2, 0, False)
+    cross_ready(cross_piece(1))
+    run_round(
+        [cross_piece(1)], [xg.at[cross_piece(1)]],
+        hooks=[functools.partial(row_arrival, 2, c, False) for c in range(1, CHUNKS - 1)],
+    )
+    here(up.at[me], u1.at[me], 1).wait()
+    scattered(u1, u1_sem)
+    pick(u1, u_pick, u_all)
+    row_arrival(2, CHUNKS - 1, False)
+    for k in range(1, groups):
+        u2_copy(k).start()
+    run_round(
+        [row_piece(2)], [xg.at[row_piece(2)]],
+        hooks=[functools.partial(row_arrival, 3, 0, False)],
+    )
+    cross_ready(cross_piece(2))
+    run_round(
+        [cross_piece(2)], [xg.at[cross_piece(2)]],
+        hooks=[functools.partial(row_arrival, 3, 1, False)],
+    )
+    for c in range(2, CHUNKS):
+        row_arrival(3, c, False)
+    run_round([row_piece(3)], [xg.at[row_piece(3)]])
+
+
+    def low_far(c):
+        at = pl.ds(c * rows, rows)
+        arrived(far, c)
+        copy = pltpu.make_async_copy(xg.at[far, span(c)], xv.at[0, at], x_sem.at[0])
+        copy.start()
+        copy.wait()
+        term = jnp.dot(xv[0, at], d_all[far], preferred_element_type=jnp.float32)
+        low[at] = low[at] + term
+        low_send(c)
+
+    def far_product(low_row, count):
+        def one(j, carry):
+            multiply([far], j, low_row, count, False)
+            return carry
+
+        lax.fori_loop(0, blocks, one, 0)
+
+    first_tiles([far])
+    for c in range(CHUNKS - 1):
+        low_far(c)
+    far_product(0, token_count - rows)
+    for c in range(CHUNKS - 1):
+        low_sum(c)
+    for k in range(1, groups):
+        u2_copy(k).wait_recv()
+    for c in range(CHUNKS - 1):
+        low_share(c)
+    first_tiles([far])
+    for c in range(CHUNKS - 2):
+        low_ready(c)
+        epilogue(c)
+    all_sent()
+    low_far(CHUNKS - 1)
+    far_product(token_count - rows, rows)
+    low_sum(CHUNKS - 1)
+    low_ready(CHUNKS - 2)
+    low_share(CHUNKS - 1)
+    epilogue(CHUNKS - 2)
+    low_ready(CHUNKS - 1)
+    epilogue(CHUNKS - 1)
+    for c in range(CHUNKS):
+        for k in range(1, n):
+            s_copy(c, k).wait_send()
+            g_copy(c, k).wait_send()
     for c in range(max(0, CHUNKS - 2), CHUNKS):
         stage_copy(c).wait()
 
@@ -770,12 +722,11 @@
     hidden = weight.shape[2]
     cols = min(BLOCK_COLS, hidden)
     twice_rank = down.shape[-1]
-    share = token_count // n
+    rows = token_count // CHUNKS
     segs = adapters.shape[1]
     dma = pltpu.SemaphoreType.DMA
     any_space = pl.BlockSpec(memory_space=pl.ANY)
     smem = pl.BlockSpec(memory_space=pltpu.SMEM)
-    block = down.shape[2:]
     leaf = up.shape[1:]
     vmem = pltpu.VMEM
     return pl.pallas_call(
@@ -788,23 +739,18 @@
         out_specs=(any_space,) * 2,
         scratch_shapes=[
             vmem((2, token_count, hidden), jnp.float32),
-            vmem((3, token_count, depth), tokens.dtype),
+            vmem((2, token_count, depth), tokens.dtype),
             vmem((2, 2, depth, 2, cols), weight.dtype),
-            vmem((groups, n // groups) + block, down.dtype),
-            vmem((n,) + block, down.dtype),
-            vmem((groups, segs) + block, down.dtype),
-            vmem((groups, segs) + block, down.dtype),
-            vmem((size,) + block, down.dtype),
+            vmem((n, depth, twice_rank), down.dtype),
+            vmem((token_count, twice_rank), jnp.float32),
             vmem((n,) + leaf, up.dtype),
             vmem((groups, segs) + leaf, up.dtype),
             vmem((groups, segs) + leaf, up.dtype),
             vmem((size,) + leaf, up.dtype),
-            vmem((size, cores, share, twice_rank), jnp.float32),
-            vmem((size, share, twice_rank), jnp.float32),
-            vmem((size, share, twice_rank), jnp.float32),
-            vmem((size, share, twice_rank), jnp.float32),
-            vmem((size, cores, share, twice_rank), jnp.bfloat16),
-            vmem((2, token_count // CHUNKS, hidden), jnp.bfloat16),
+            vmem((CHUNKS, n, rows // n, twice_rank), jnp.bfloat16),
+            vmem((CHUNKS, n, rows // n, twice_rank), jnp.bfloat16),
+            vmem((CHUNKS, n, rows // n, twice_rank), jnp.bfloat16),
+            vmem((2, rows, hidden), jnp.bfloat16),
             dma((n, CHUNKS)),
             dma((n, CHUNKS)),
             dma((n, CHUNKS)),
@@ -815,12 +761,8 @@
             dma((2, n)),
             dma((2, groups)),
             dma((2, size)),
-            dma((2, n)),
-            dma((2, groups)),
-            dma((2, size)),
-            dma((4,)),
-            dma((2, size)),
-            dma((2, size)),
+            dma((2, CHUNKS, n)),
+            dma((2, CHUNKS, n)),
             dma((6,)),
         ],
         compiler_params=pltpu.CompilerParams(
@@ -841,11 +783,8 @@
 ):
     groups = lax.axis_size("grp")
     size, cores = lax.axis_size("tp"), lax.axis_size("cores")
-    n = size * cores
     depth = tokens.shape[1]
-    down = down_factor_pool.reshape(
-        n // groups, groups, depth // groups, down_factor_pool.shape[2]
-    )
+    down = down_factor_pool.reshape(size * cores // groups, depth, down_factor_pool.shape[2])
     up = up_factor_pool.reshape(up_factor_pool.shape[2:])
     return fused_call(
         segment_tile_counts,
@@ -863,7 +802,7 @@
 
 def fits(mesh):
     size, cores, groups = mesh.shape["tp"], mesh.shape["cores"], mesh.shape["grp"]
-    return cores == 2 and size == groups and (size * cores) % groups == 0 and size == 4
+    return cores == 2 and size == 4 and size * cores % groups == 0
 
 
 def per_device(*args):

time: 302 us -> 248 us (0.82)
  Pallas kernels: 296 us -> 243 us
    pallas_call x1, Pallas kernels: 296 us -> 243 us  [fused_call(): pl.pallas_call(fused_kernel, out_shape=(jax.ShapeDtypeStruct((n, token_co...]
where the time goes in v2:
time: 248 us
  Pallas kernels  243 us (98%)
  local copies, waits for them, and re-layouts  4.79 us (2%)
    pallas_call x1, Pallas kernels, fused_call(): pl.pallas_call(fused_kernel, out_shape=(jax.ShapeDtypeStruct((n, token_co...  243 us

profile of v2, /device:TPU:0, one launch (start us, length us, event | category | flops | bytes accessed | tf_op | source)
XLA Modules:
  0.0 247.6 jit_solution(6367364611556215073)
XLA Ops:
  0.0 242.8 %fused.1 = (bf16[8,1024,1024]{2,1,0:T(8,128)(2,1)}, bf16[1024,2048]{1,0:T(8,128)(2,1)}) custom-call(s32[1,3]{1,0:T(1,128)} %counts.1, s32[4,3]{1,0:T(4,128)} %adapters.1, s32[8]{0:T(128)} %pool_rows.1, bf16[1024,1024]{1,0:T(8,128)(2,1)} %tokens.1, bf16[8192,2,2048]{2,1,0:T(2,128)(2,1)} %weight.1, bf16[2,1024,256]{2,1,0:T(8,128)(2,1)} %bitcast.3, ...), custom_call_target="tpu_custom_call" | custom-call | tf_op jit(solution)/shard_map/fused/pallas_call | solution.py:732
  242.8 4.8 %copy.9 = bf16[1024,2048]{1,0:T(8,128)(2,1)} copy(bf16[1024,2048]{1,0:T(8,128)(2,1)} %get-tuple-element.6) | data formatting | bytes 8388608

commit v3 on v2

--- a/solution.py
+++ b/solution.py
@@ -157,7 +157,7 @@
 MESH = pl.DeviceIdType.MESH
 CHUNKS = 4
 END_SHIFT = 0
-BLOCK_COLS = 256
+BLOCK_COLS = 512
 
 
 def table(rows, i, k):
@@ -345,9 +345,6 @@
         for k, piece in enumerate(pieces):
             w_copy(piece, 0, 0, k).start()
 
-    def x_copy(src, k):
-        return pltpu.make_async_copy(src, xv.at[k], x_sem.at[k])
-
     def multiply(pieces, j, low_row, count, first):
         slot = lax.rem(j, 2)
 
@@ -368,23 +365,29 @@
                 total = term if total is None else total + term
             acc[h, where, at] = total
 
-    def run_round(pieces, sources, first=False, project=True, hooks=()):
+    def run_round(pieces, sources, first=False, project=True, hooks=(), start=0, count=None):
+        count = token_count if count is None else count
+        at = pl.ds(start, count)
         first_tiles(pieces)
-        copies = [x_copy(src, k) for k, src in enumerate(sources)]
+        copies = [
+            pltpu.make_async_copy(src.at[at], xv.at[k, at], x_sem.at[k])
+            for k, src in enumerate(sources)
+        ]
         for copy in copies:
             copy.start()
         for copy in copies:
             copy.wait()
         if project:
             for k, piece in enumerate(pieces):
-                low[...] = low[...] + jnp.dot(
-                    xv[k], d_all[piece], preferred_element_type=jnp.float32
+                low[at] = low[at] + jnp.dot(
+                    xv[k, at], d_all[piece], preferred_element_type=jnp.float32
                 )
 
         def one(j, carry):
-            multiply(pieces, j, 0, token_count, first)
+            multiply(pieces, j, start, count, first)
             for i, hook in enumerate(hooks):
-                pl.when(j == (i + 1) * blocks // len(hooks) - 1)(hook)
+                if hook is not None:
+                    pl.when(j == (i + 1) * blocks // len(hooks) - 1)(hook)
             return carry
 
         lax.fori_loop(0, blocks, one, 0)
@@ -663,9 +666,11 @@
         [cross_piece(2)], [xg.at[cross_piece(2)]],
         hooks=[functools.partial(row_arrival, 3, 1, False)],
     )
-    for c in range(2, CHUNKS):
-        row_arrival(3, c, False)
-    run_round([row_piece(3)], [xg.at[row_piece(3)]])
+    top = token_count // 2
+    run_round(
+        [row_piece(3)], [xg.at[row_piece(3)]], start=0, count=top,
+        hooks=[functools.partial(row_arrival, 3, 2, False)],
+    )
 
 
     def low_far(c):
@@ -678,41 +683,50 @@
         low[at] = low[at] + term
         low_send(c)
 
-    def far_product(low_row, count):
+    def far_product(low_row, count, hook=None):
         def one(j, carry):
             multiply([far], j, low_row, count, False)
+            if hook is not None:
+                pl.when(j == blocks // 2 - 1)(hook)
             return carry
 
         lax.fori_loop(0, blocks, one, 0)
 
     first_tiles([far])
-    for c in range(CHUNKS - 1):
-        low_far(c)
-    far_product(0, token_count - rows)
-    for c in range(CHUNKS - 1):
-        low_sum(c)
+    low_far(0)
+    low_far(1)
+    far_product(0, top, functools.partial(row_arrival, 3, 3, False))
+    run_round([row_piece(3)], [xg.at[row_piece(3)]], start=top, count=top)
+    first_tiles([far])
+    low_sum(0)
+    low_sum(1)
+    low_far(2)
+    low_share(0)
+    low_share(1)
+    far_product(top, rows)
     for k in range(1, groups):
         u2_copy(k).wait_recv()
-    for c in range(CHUNKS - 1):
-        low_share(c)
     first_tiles([far])
-    for c in range(CHUNKS - 2):
-        low_ready(c)
-        epilogue(c)
+    low_sum(2)
+    low_ready(0)
+    epilogue(0)
+    low_share(2)
+    low_ready(1)
+    epilogue(1)
+    low_far(3)
+    far_product(top + rows, rows)
+    low_sum(3)
+    low_ready(2)
+    low_share(3)
+    epilogue(2)
     all_sent()
-    low_far(CHUNKS - 1)
-    far_product(token_count - rows, rows)
-    low_sum(CHUNKS - 1)
-    low_ready(CHUNKS - 2)
-    low_share(CHUNKS - 1)
-    epilogue(CHUNKS - 2)
-    low_ready(CHUNKS - 1)
-    epilogue(CHUNKS - 1)
+    low_ready(3)
+    epilogue(3)
     for c in range(CHUNKS):
         for k in range(1, n):
             s_copy(c, k).wait_send()
             g_copy(c, k).wait_send()
-    for c in range(max(0, CHUNKS - 2), CHUNKS):
+    for c in range(CHUNKS - 2, CHUNKS):
         stage_copy(c).wait()
 
 

time: 248 us -> 237 us (0.956)
  Pallas kernels: 243 us -> 232 us
    pallas_call x1, Pallas kernels: 243 us -> 232 us  [fused_call(): pl.pallas_call(fused_kernel, out_shape=(jax.ShapeDtypeStruct((n, token_co...]
where the time goes in v3:
time: 237 us
  Pallas kernels  232 us (98%)
  local copies, waits for them, and re-layouts  4.79 us (2%)
    pallas_call x1, Pallas kernels, fused_call(): pl.pallas_call(fused_kernel, out_shape=(jax.ShapeDtypeStruct((n, token_co...  232 us
    unnamed x1, local copies, waits for them, and re-layouts  4.79 us

profile of v3, /device:TPU:0, one launch (start us, length us, event | category | flops | bytes accessed | tf_op | source)
XLA Modules:
  0.0 236.6 jit_solution(12862600441967587223)
XLA Ops:
  0.0 231.8 %fused.1 = (bf16[8,1024,1024]{2,1,0:T(8,128)(2,1)}, bf16[1024,2048]{1,0:T(8,128)(2,1)}) custom-call(s32[1,3]{1,0:T(1,128)} %counts.1, s32[4,3]{1,0:T(4,128)} %adapters.1, s32[8]{0:T(128)} %pool_rows.1, bf16[1024,1024]{1,0:T(8,128)(2,1)} %tokens.1, bf16[8192,2,2048]{2,1,0:T(2,128)(2,1)} %weight.1, bf16[2,1024,256]{2,1,0:T(8,128)(2,1)} %bitcast.3, ...), custom_call_target="tpu_custom_call" | custom-call | tf_op jit(solution)/shard_map/fused/pallas_call | solution.py:746
  231.9 4.8 %copy.9 = bf16[1024,2048]{1,0:T(8,128)(2,1)} copy(bf16[1024,2048]{1,0:T(8,128)(2,1)} %get-tuple-element.6) | data formatting | bytes 8388608

commit v4 on v3

--- a/solution.py
+++ b/solution.py
@@ -345,8 +345,12 @@
         for k, piece in enumerate(pieces):
             w_copy(piece, 0, 0, k).start()
 
-    def multiply(pieces, j, low_row, count, first):
+    def multiply(pieces, j, low_row, count, first, then):
         slot = lax.rem(j, 2)
+
+        @pl.when(j + 1 == blocks)
+        def _():
+            first_tiles(then)
 
         @pl.when(j + 1 < blocks)
         def _():
@@ -365,10 +369,9 @@
                 total = term if total is None else total + term
             acc[h, where, at] = total
 
-    def run_round(pieces, sources, first=False, project=True, hooks=(), start=0, count=None):
+    def run_round(pieces, sources, then, first=False, project=True, hooks=(), start=0, count=None):
         count = token_count if count is None else count
         at = pl.ds(start, count)
-        first_tiles(pieces)
         copies = [
             pltpu.make_async_copy(src.at[at], xv.at[k, at], x_sem.at[k])
             for k, src in enumerate(sources)
@@ -382,9 +385,11 @@
                 low[at] = low[at] + jnp.dot(
                     xv[k, at], d_all[piece], preferred_element_type=jnp.float32
                 )
-
+        products(pieces, then, first, hooks, start, count)
+
+    def products(pieces, then, first, hooks, start, count):
         def one(j, carry):
-            multiply(pieces, j, start, count, first)
+            multiply(pieces, j, start, count, first, then)
             for i, hook in enumerate(hooks):
                 if hook is not None:
                     pl.when(j == (i + 1) * blocks // len(hooks) - 1)(hook)
@@ -634,21 +639,22 @@
     here(down, d_all.at[pl.ds(g * per, per)], 0).start()
     here(up.at[me], u1.at[me], 1).start()
     u_scatter(started)
+    first_tiles([me])
+    pair = [row_piece(1), cross_piece(0)]
     run_round(
-        [me], [tokens], True, False,
+        [me], [tokens], pair, True, False,
         [functools.partial(near_arrivals, c) for c in range(CHUNKS)],
     )
     here(down, d_all.at[pl.ds(g * per, per)], 0).wait()
     for k in range(1, groups):
         d_copy(k).wait_recv()
     low[...] = jnp.dot(xv[0], d_all[me], preferred_element_type=jnp.float32)
-    pair = [row_piece(1), cross_piece(0)]
-    run_round(pair, [xg.at[q] for q in pair])
+    run_round(pair, [xg.at[q] for q in pair], [cross_piece(1)])
     pass_on(u1, u_relay, u1_sem, ur_sem)
     row_arrival(2, 0, False)
     cross_ready(cross_piece(1))
     run_round(
-        [cross_piece(1)], [xg.at[cross_piece(1)]],
+        [cross_piece(1)], [xg.at[cross_piece(1)]], [row_piece(2)],
         hooks=[functools.partial(row_arrival, 2, c, False) for c in range(1, CHUNKS - 1)],
     )
     here(up.at[me], u1.at[me], 1).wait()
@@ -657,18 +663,19 @@
     row_arrival(2, CHUNKS - 1, False)
     for k in range(1, groups):
         u2_copy(k).start()
+    near = row_piece(size - 1)
     run_round(
-        [row_piece(2)], [xg.at[row_piece(2)]],
+        [row_piece(2)], [xg.at[row_piece(2)]], [cross_piece(2)],
         hooks=[functools.partial(row_arrival, 3, 0, False)],
     )
     cross_ready(cross_piece(2))
     run_round(
-        [cross_piece(2)], [xg.at[cross_piece(2)]],
-        hooks=[functools.partial(row_arrival, 3, 1, False)],
+        [cross_piece(2)], [xg.at[cross_piece(2)]], [near],
+        hooks=[None, None, functools.partial(row_arrival, 3, 1, False), None],
     )
     top = token_count // 2
     run_round(
-        [row_piece(3)], [xg.at[row_piece(3)]], start=0, count=top,
+        [near], [xg.at[near]], [far], start=0, count=top,
         hooks=[functools.partial(row_arrival, 3, 2, False)],
     )
 
@@ -683,43 +690,32 @@
         low[at] = low[at] + term
         low_send(c)
 
-    def far_product(low_row, count, hook=None):
-        def one(j, carry):
-            multiply([far], j, low_row, count, False)
-            if hook is not None:
-                pl.when(j == blocks // 2 - 1)(hook)
-            return carry
-
-        lax.fori_loop(0, blocks, one, 0)
-
-    first_tiles([far])
     low_far(0)
     low_far(1)
-    far_product(0, top, functools.partial(row_arrival, 3, 3, False))
-    run_round([row_piece(3)], [xg.at[row_piece(3)]], start=top, count=top)
-    first_tiles([far])
+    products(
+        [far], [near], False, [functools.partial(row_arrival, 3, 3, False), None], 0, top
+    )
+    run_round([near], [xg.at[near]], [far], start=top, count=top)
+    low_far(2)
     low_sum(0)
     low_sum(1)
-    low_far(2)
+    for k in range(1, groups):
+        u2_copy(k).wait_recv()
     low_share(0)
     low_share(1)
-    far_product(top, rows)
-    for k in range(1, groups):
-        u2_copy(k).wait_recv()
-    first_tiles([far])
-    low_sum(2)
+    low_far(3)
+    products([far], [], False, (), top, top)
+    for c in range(2, CHUNKS):
+        low_sum(c)
     low_ready(0)
+    low_share(2)
+    low_share(3)
     epilogue(0)
-    low_share(2)
     low_ready(1)
     epilogue(1)
-    low_far(3)
-    far_product(top + rows, rows)
-    low_sum(3)
+    all_sent()
     low_ready(2)
-    low_share(3)
     epilogue(2)
-    all_sent()
     low_ready(3)
     epilogue(3)
     for c in range(CHUNKS):

time: 237 us -> 229 us (0.966)
  Pallas kernels: 232 us -> 224 us
    pallas_call x1, Pallas kernels: 232 us -> 224 us  [fused_call(): pl.pallas_call(fused_kernel, out_shape=(jax.ShapeDtypeStruct((n, token_co...]
where the time goes in v4:
time: 229 us; the launch traced here: 228 us
  Pallas kernels  224 us (98%)
  local copies, waits for them, and re-layouts  4.79 us (2%)
    pallas_call x1, Pallas kernels, fused_call(): pl.pallas_call(fused_kernel, out_shape=(jax.ShapeDtypeStruct((n, token_co...  224 us
    unnamed x1, local copies, waits for them, and re-layouts  4.79 us

profile of v4, /device:TPU:0, one launch (start us, length us, event | category | flops | bytes accessed | tf_op | source)
XLA Modules:
  0.0 228.4 jit_solution(14830244833622146344)
XLA Ops:
  0.0 223.6 %fused.1 = (bf16[8,1024,1024]{2,1,0:T(8,128)(2,1)}, bf16[1024,2048]{1,0:T(8,128)(2,1)}) custom-call(s32[1,3]{1,0:T(1,128)} %counts.1, s32[4,3]{1,0:T(4,128)} %adapters.1, s32[8]{0:T(128)} %pool_rows.1, bf16[1024,1024]{1,0:T(8,128)(2,1)} %tokens.1, bf16[8192,2,2048]{2,1,0:T(2,128)(2,1)} %weight.1, bf16[2,1024,256]{2,1,0:T(8,128)(2,1)} %bitcast.3, ...), custom_call_target="tpu_custom_call" | custom-call | tf_op jit(solution)/shard_map/fused/pallas_call | solution.py:742
  223.6 4.8 %copy.9 = bf16[1024,2048]{1,0:T(8,128)(2,1)} copy(bf16[1024,2048]{1,0:T(8,128)(2,1)} %get-tuple-element.6) | data formatting | bytes 8388608

commit v5 on v4

--- a/solution.py
+++ b/solution.py
@@ -649,25 +649,27 @@
     for k in range(1, groups):
         d_copy(k).wait_recv()
     low[...] = jnp.dot(xv[0], d_all[me], preferred_element_type=jnp.float32)
-    run_round(pair, [xg.at[q] for q in pair], [cross_piece(1)])
-    pass_on(u1, u_relay, u1_sem, ur_sem)
+    run_round(
+        pair, [xg.at[q] for q in pair], [cross_piece(1)],
+        hooks=[None, None, functools.partial(pass_on, u1, u_relay, u1_sem, ur_sem), None],
+    )
     row_arrival(2, 0, False)
     cross_ready(cross_piece(1))
     run_round(
         [cross_piece(1)], [xg.at[cross_piece(1)]], [row_piece(2)],
         hooks=[functools.partial(row_arrival, 2, c, False) for c in range(1, CHUNKS - 1)],
     )
-    here(up.at[me], u1.at[me], 1).wait()
-    scattered(u1, u1_sem)
-    pick(u1, u_pick, u_all)
     row_arrival(2, CHUNKS - 1, False)
-    for k in range(1, groups):
-        u2_copy(k).start()
     near = row_piece(size - 1)
     run_round(
         [row_piece(2)], [xg.at[row_piece(2)]], [cross_piece(2)],
         hooks=[functools.partial(row_arrival, 3, 0, False)],
     )
+    here(up.at[me], u1.at[me], 1).wait()
+    scattered(u1, u1_sem)
+    pick(u1, u_pick, u_all)
+    for k in range(1, groups):
+        u2_copy(k).start()
     cross_ready(cross_piece(2))
     run_round(
         [cross_piece(2)], [xg.at[cross_piece(2)]], [near],

time: 229 us -> 229 us (level)
  no operation moved by 1% of the time
where the time goes in v5:
time: 229 us; the launch traced here: 228 us
  Pallas kernels  224 us (98%)
  local copies, waits for them, and re-layouts  4.79 us (2%)
    pallas_call x1, Pallas kernels, fused_call(): pl.pallas_call(fused_kernel, out_shape=(jax.ShapeDtypeStruct((n, token_co...  224 us
    unnamed x1, local copies, waits for them, and re-layouts  4.79 us

profile of v5, /device:TPU:0, one launch (start us, length us, event | category | flops | bytes accessed | tf_op | source)
XLA Modules:
  0.0 228.4 jit_solution(14609442832858887909)
XLA Ops:
  0.0 223.6 %fused.1 = (bf16[8,1024,1024]{2,1,0:T(8,128)(2,1)}, bf16[1024,2048]{1,0:T(8,128)(2,1)}) custom-call(s32[1,3]{1,0:T(1,128)} %counts.1, s32[4,3]{1,0:T(4,128)} %adapters.1, s32[8]{0:T(128)} %pool_rows.1, bf16[1024,1024]{1,0:T(8,128)(2,1)} %tokens.1, bf16[8192,2,2048]{2,1,0:T(2,128)(2,1)} %weight.1, bf16[2,1024,256]{2,1,0:T(8,128)(2,1)} %bitcast.3, ...), custom_call_target="tpu_custom_call" | custom-call | tf_op jit(solution)/shard_map/fused/pallas_call | solution.py:744
  223.6 4.8 %copy.9 = bf16[1024,2048]{1,0:T(8,128)(2,1)} copy(bf16[1024,2048]{1,0:T(8,128)(2,1)} %get-tuple-element.6) | data formatting | bytes 8388608
